TPU v7x, 32 devices: a whole 2x2x4 slice. The times are simulated.
32 devices in a mesh: groups: 2 (over y), tm: 4 (over z), zoom: 2 (over x), pol: 2 (over core).
Axes of the slice: x: 2, y: 2, z: 4, core: 2. Of those that a mesh axis runs over, the one named last changes fastest.
Arguments:
- voltages: bfloat16 [2, 4, 7464960], P('pol', 'groups', ('tm', 'zoom')), parts along dimension 1, may hold values from -6 to 6
- section1_taps: float32 [12, 512], replicated, may hold values from -0.078125 to 0.078125
- section2_taps: float32 [5, 3456], replicated, may hold values from -0.046875 to 0.046875
- band_starts: int32 [4], P('groups'), parts along dimension 0, may hold values from 0 to 511
- band_widths: int32 [4], P('groups'), parts along dimension 0, may hold values from 1 to 20, 24 in all
Outputs:
- fine: float32 [2, 2, 4, 1, 58320], P('pol', 'zoom', 'groups', None, 'tm'), parts along dimension 2
There are 2 independent parts, one for each index of `groups`. A program takes and returns all parts, laid end to end along the dimension named above; an argument that names none is the same for every part. Nothing has to cross between parts.
Inputs may be any that keep to these rules, and one draw needn't show every extreme that they name: `band_widths`: the 2 widths sum to 24, and one band has exactly 20 coarse channels.
All inputs are finite; a program needn't handle non-finite values.
Results may differ from a plain program's by a relative error of at most 0.0069.
Values may be sent and summed in bfloat16 or wider, within the bound.
A program may use at most 192 MiB of HBM per device.

v0:
```python
import math

import jax
import jax.numpy as jnp
import numpy as np
from jax import lax
from jax.sharding import PartitionSpec as P

HOP = 432
FA = 27
FB = 128
KEEP = 2916
EDGE = 128
CH_DEV = 5
LIVE_DEV = 3


def shifted(value, axis, steps):
    count = lax.axis_size(axis)
    initial, last = (max(0, -steps), min(count, count - steps))
    return lax.ppermute(value, axis, [(source, source + steps) for source in range(initial, last)])


def with_halo(value, sides, width):
    for axis, dim in sides:
        count, length = (lax.axis_size(axis), value.shape[dim])
        up = [(i, (i + 1) % count) for i in range(count - 1)]
        down = [(j, i) for i, j in up]
        last = lax.slice_in_dim(value, length - width, length, axis=dim)
        initial = lax.slice_in_dim(value, 0, width, axis=dim)
        before = lax.ppermute(last, axis, up)
        after = lax.ppermute(initial, axis, down)
        value = jnp.concatenate([before, value, after], axis=dim)
    return value


def angle_table(rows, cols, length):
    product = (
        jnp.arange(rows, dtype=jnp.int32)[:, None]
        * jnp.arange(cols, dtype=jnp.int32)[None, :]
        % length
    )
    return product.astype(jnp.float32) * (2.0 * math.pi / length)


def rotation_block(length):
    angles = angle_table(length, length, length)
    cosine_tab = jnp.cos(angles).astype(jnp.bfloat16)
    sine_tab = jnp.sin(angles).astype(jnp.bfloat16)
    return jnp.stack([jnp.stack([cosine_tab, sine_tab]), jnp.stack([-sine_tab, cosine_tab])])


def joined_table(length):
    angles = angle_table(length, length, length)
    cosine_tab = jnp.cos(angles).astype(jnp.bfloat16)
    sine_tab = jnp.sin(angles).astype(jnp.bfloat16)
    top_rows = jnp.concatenate([cosine_tab, -sine_tab], axis=1)
    bottom_rows = jnp.concatenate([sine_tab, cosine_tab], axis=1)
    return jnp.concatenate([top_rows, bottom_rows], axis=0)


def bin_index(radix_a, radix_b, keep_len, edge_len):
    fine_len = radix_a * radix_b
    offsets = (np.arange(keep_len + 2 * edge_len) - keep_len // 2 - edge_len) % fine_len
    base = offsets % radix_a * (2 * radix_b) + offsets // radix_a
    return (base, base + radix_b)


def frame_view(segment, spectra, chan_len, hop_len):
    pieces = -(-chan_len // hop_len)
    framed = segment[:, : (spectra + pieces - 1) * hop_len].reshape(
        segment.shape[0], spectra + pieces - 1, hop_len
    )
    joined = jnp.concatenate(
        [framed[:, offset : offset + spectra] for offset in range(pieces)], axis=2
    )
    return joined[:, :, :chan_len]


def weighted_frames(signal, taps, spectra, hop_len):
    chan_len = taps.shape[1]
    running = jnp.zeros((2, spectra, chan_len), jnp.float32)
    for tap_index in range(taps.shape[0]):
        frames = frame_view(signal[:, tap_index * chan_len :], spectra, chan_len, hop_len)
        running = running + taps[tap_index][None, None, :] * frames.astype(jnp.float32)
    return running.astype(jnp.bfloat16)


def fine_spectra(series, section2_taps, radix_a, radix_b, keep_len, edge_len):
    tap_count, fine_len = section2_taps.shape
    items = series.shape[1]
    row_count = series.shape[2] // fine_len
    spectra = row_count - tap_count + 1
    row_blocks = series.reshape(2, items, row_count, fine_len)
    running = jnp.zeros((2, items, spectra, fine_len), jnp.float32)
    for tap_index in range(tap_count):
        running = running + section2_taps[tap_index] * row_blocks[
            :, :, tap_index : tap_index + spectra
        ].astype(jnp.float32)
    weighted = running.astype(jnp.bfloat16).reshape(2, items, spectra, radix_a, radix_b)
    partial_value = jnp.einsum(
        "pqkm,qcfmb->pcfkb", rotation_block(radix_a), weighted, preferred_element_type=jnp.float32
    )
    angles = angle_table(radix_a, radix_b, fine_len)
    cosine_tab = jnp.cos(angles)
    sine_tab = jnp.sin(angles)
    real_part = partial_value[0] * cosine_tab + partial_value[1] * sine_tab
    imag_part = partial_value[1] * cosine_tab - partial_value[0] * sine_tab
    twiddled = jnp.concatenate([real_part, imag_part], axis=-1).astype(jnp.bfloat16)
    spectrum = jnp.einsum(
        "cfkm,mj->cfkj", twiddled, joined_table(radix_b), preferred_element_type=jnp.float32
    )
    flattened = spectrum.reshape(items, spectra, radix_a * 2 * radix_b)
    real_index, imag_index = bin_index(radix_a, radix_b, keep_len, edge_len)
    return jnp.stack(
        [jnp.take(flattened, real_index, axis=2), jnp.take(flattened, imag_index, axis=2)]
    )


def stitch_bands(extended, upper_rim, lower_rim, slot_ids, band_width, keep_len, edge_len):
    centre = extended[..., edge_len : edge_len + keep_len]
    live = (slot_ids < band_width).astype(jnp.float32)[None, :, None, None]
    upper_ok = (slot_ids + 1 < band_width).astype(jnp.float32)[None, :, None, None]
    lower_ok = ((slot_ids >= 1) & (slot_ids < band_width)).astype(jnp.float32)[None, :, None, None]
    ramp = (jnp.arange(edge_len, dtype=jnp.float32) + 0.5) / (2.0 * edge_len)
    upper_weight = ramp * upper_ok
    lower_weight = ramp[::-1] * lower_ok
    low_part = centre[..., :edge_len] * (1.0 - lower_weight) + lower_rim * lower_weight
    high_part = centre[..., keep_len - edge_len :] * (1.0 - upper_weight) + upper_rim * upper_weight
    joined = jnp.concatenate(
        [low_part, centre[..., edge_len : keep_len - edge_len], high_part], axis=-1
    )
    return joined * live


def on_device(voltages, section1_taps, section2_taps, band_starts, band_widths):
    signal = voltages[0]
    tap_count, chan_len = section1_taps.shape
    spectra = signal.shape[1] // HOP
    rim_len = tap_count * chan_len - HOP
    pieces = -(-chan_len // HOP)
    following = shifted(signal[:, :rim_len], ("tm", "zoom"), -1)
    padded = jnp.concatenate(
        [signal, following, jnp.zeros((2, pieces * HOP), jnp.bfloat16)], axis=1
    )
    weighted = weighted_frames(padded, section1_taps, spectra, HOP)
    coarse = jnp.einsum(
        "pqkn,qsn->pks", rotation_block(chan_len), weighted, preferred_element_type=jnp.float32
    ).astype(jnp.bfloat16)
    tm_count = lax.axis_size("tm")
    zoom_count = lax.axis_size("zoom")
    slot_local = jnp.arange(CH_DEV, dtype=jnp.int32)
    slot_ids = lax.axis_index("tm") * CH_DEV + slot_local
    band_count = band_widths.shape[0]
    band_ids = jnp.arange(band_count, dtype=jnp.int32)
    my_band = band_ids == lax.axis_index("zoom")
    band_width = jnp.sum(jnp.where(my_band, band_widths, 0))
    device_count = tm_count * zoom_count
    live_count = LIVE_DEV * device_count
    band_ends = jnp.cumsum(band_widths)
    band_firsts = band_ends - band_widths
    live_ids = jnp.arange(live_count, dtype=jnp.int32)
    band_of = jnp.sum((band_ends[None, :] <= live_ids[:, None]).astype(jnp.int32), axis=1)
    member = band_of[:, None] == band_ids[None, :]
    first_of = jnp.sum(jnp.where(member, band_firsts[None, :], 0), axis=1)
    start_of = jnp.sum(jnp.where(member, band_starts[None, :], 0), axis=1)
    live_channels = (start_of + live_ids - first_of) % chan_len
    packed_order = live_channels.reshape(device_count, LIVE_DEV).T.reshape(-1)
    packed = jnp.take(coarse, packed_order, axis=1).reshape(2, LIVE_DEV, device_count, spectra)
    received = lax.all_to_all(packed, ("tm", "zoom"), split_axis=2, concat_axis=2, tiled=True)
    series = received.reshape(2, received.shape[1], -1)
    computed = fine_spectra(series, section2_taps, FA, FB, KEEP, EDGE)
    wanted = jnp.sum(jnp.where(my_band, band_firsts, 0)) + slot_ids
    valid = slot_ids < band_width
    piece = lax.all_gather(computed, ("tm", "zoom"), axis=1, tiled=True)
    piece_ids = jnp.arange(piece.shape[1], dtype=jnp.int32)
    chosen = ((wanted[:, None] == piece_ids[None, :]) & valid[:, None]).astype(jnp.float32)
    extended = jnp.einsum("kn,pnfx->pkfx", chosen, piece, precision=lax.Precision.HIGHEST)
    seam_rows = jnp.concatenate([extended[..., :EDGE], extended[..., KEEP + EDGE :]], axis=-1)
    widened = with_halo(seam_rows, (("tm", 1),), 1)
    upper_rim = widened[:, 2:, :, :EDGE]
    lower_rim = widened[:, :CH_DEV, :, EDGE:]
    stitched = stitch_bands(extended, upper_rim, lower_rim, slot_ids, band_width, KEEP, EDGE)
    fine_count = stitched.shape[2]
    result = jnp.transpose(stitched, (0, 2, 1, 3)).reshape(2, fine_count, CH_DEV * KEEP)
    return result[None, None]


def solution(mesh):
    placed = (P("pol", "groups", ("tm", "zoom")), P(), P(), P("groups"), P("groups"))
    return jax.shard_map(
        on_device,
        mesh=mesh,
        in_specs=placed,
        out_specs=P("pol", "zoom", "groups", None, "tm"),
        check_vma=False,
    )
```

profile of v0, /device:TPU:0, one launch (start us, length us, event | category | flops | bytes accessed | tf_op | source)
XLA Modules:
  0.0 742.4 jit_solution(14112968930927286851)
XLA Ops:
  0.8 1.4 collective-permute-start
  2.2 7.9 %constant_dynamic-update-slice_fusion = bf16[2,939696]{1,0:T(2,128)(2,1)} fusion(bf16[1,2,933120]{2,1,0:T(2,128)(2,1)} %param.9), kind=kLoop, calls=%fused_computation.148 | loop fusion | bytes 7464960
  10.2 4.3 sine_convert_fusion
  14.5 4.0 fusion.22
  19.4 0.9 sine_convert_fusion.1
  20.3 0.9 fusion.54
  24.4 1.2 fusion.76
  25.7 1.1 compare_convert_fusion
  27.6 1.1 maximum_bitcast_fusion
  30.5 136.5 %fusion.2 = (bf16[2,933552]{1,0:T(2,128)(2,1)}, bf16[2,933552]{1,0:T(2,128)(2,1)}, bf16[2,933552]{1,0:T(2,128)(2,1)}, bf16[2,933552]{1,0:T(2,128)(2,1)}, bf16[2,...) fusion(bf16[2,5712]{1,0:T(2,128)(2,1)S(1)} %collective-permute-done, bf16[2,933120]{1,0:T(2,128)(2,1)} %bitcast.123), kind=kLoop, calls=%fused_computation.30 | loop fusion | flops 44810496 | bytes 26160576 | tf_op jit(solution)/shard_map/concatenate | solution.py:143
  167.1 9.1 %reshape.688 = bf16[1867104]{0:T(1024)(128)(2,1)} reshape(bf16[2,933552]{1,0:T(2,128)(2,1)} %get-tuple-element.43) | data formatting | bytes 7468416
  176.2 13.3 %reshape.600 = bf16[2,2161,432]{2,1,0:T(8,128)(2,1)} reshape(bf16[1867104]{0:T(1024)(128)(2,1)} %reshape.688) | data formatting | bytes 7468416 | tf_op jit(solution)/shard_map/reshape | solution.py:71
  189.5 9.1 %reshape.686 = bf16[1867104]{0:T(1024)(128)(2,1)} reshape(bf16[2,933552]{1,0:T(2,128)(2,1)} %get-tuple-element.44) | data formatting | bytes 7468416
  198.6 13.1 %reshape.601 = bf16[2,2161,432]{2,1,0:T(8,128)(2,1)} reshape(bf16[1867104]{0:T(1024)(128)(2,1)} %reshape.686) | data formatting | bytes 7468416 | tf_op jit(solution)/shard_map/reshape | solution.py:71
  211.7 9.1 %reshape.684 = bf16[1867104]{0:T(1024)(128)(2,1)} reshape(bf16[2,933552]{1,0:T(2,128)(2,1)} %get-tuple-element.45) | data formatting | bytes 7468416
  220.9 13.1 %reshape.602 = bf16[2,2161,432]{2,1,0:T(8,128)(2,1)} reshape(bf16[1867104]{0:T(1024)(128)(2,1)} %reshape.684) | data formatting | bytes 7468416 | tf_op jit(solution)/shard_map/reshape | solution.py:71
  234.0 9.1 %reshape.682 = bf16[1867104]{0:T(1024)(128)(2,1)} reshape(bf16[2,933552]{1,0:T(2,128)(2,1)} %get-tuple-element.46) | data formatting | bytes 7468416
  243.1 13.4 %reshape.603 = bf16[2,2161,432]{2,1,0:T(8,128)(2,1)} reshape(bf16[1867104]{0:T(1024)(128)(2,1)} %reshape.682) | data formatting | bytes 7468416 | tf_op jit(solution)/shard_map/reshape | solution.py:71
  256.5 9.3 %reshape.680 = bf16[1867104]{0:T(1024)(128)(2,1)} reshape(bf16[2,933552]{1,0:T(2,128)(2,1)} %get-tuple-element.47) | data formatting | bytes 7468416
  265.7 12.9 %reshape.604 = bf16[2,2161,432]{2,1,0:T(8,128)(2,1)} reshape(bf16[1867104]{0:T(1024)(128)(2,1)} %reshape.680) | data formatting | bytes 7468416 | tf_op jit(solution)/shard_map/reshape | solution.py:71
  278.7 9.6 %reshape.678 = bf16[1867104]{0:T(1024)(128)(2,1)} reshape(bf16[2,933552]{1,0:T(2,128)(2,1)} %get-tuple-element.48) | data formatting | bytes 7468416
  288.3 12.9 %reshape.605 = bf16[2,2161,432]{2,1,0:T(8,128)(2,1)} reshape(bf16[1867104]{0:T(1024)(128)(2,1)} %reshape.678) | data formatting | bytes 7468416 | tf_op jit(solution)/shard_map/reshape | solution.py:71
  301.2 106.8 %fusion.8 = (bf16[2,933552]{1,0:T(2,128)(2,1)}, bf16[2,933552]{1,0:T(2,128)(2,1)}, bf16[2,933552]{1,0:T(2,128)(2,1)}, bf16[2,933552]{1,0:T(2,128)(2,1)}, bf16[2,933552]{1,0:T(2,128)(2,1)}) fusion(bf16[2,5712]{1,0:T(2,128)(2,1)S(1)} %collective-permute-done, bf16[2,933120]{1,0:T(2,128)(2,1)} %bitcast.124), kind=kLoop, calls=%fused_computation.36 | loop fusion | flops 37342080 | bytes 22426368 | tf_op jit(solution)/shard_map/concatenate | solution.py:143
  408.0 9.1 %reshape.676 = bf16[1867104]{0:T(1024)(128)(2,1)} reshape(bf16[2,933552]{1,0:T(2,128)(2,1)} %get-tuple-element.49) | data formatting | bytes 7468416
  417.1 13.2 %reshape.606 = bf16[2,2161,432]{2,1,0:T(8,128)(2,1)} reshape(bf16[1867104]{0:T(1024)(128)(2,1)} %reshape.676) | data formatting | bytes 7468416 | tf_op jit(solution)/shard_map/reshape | solution.py:71
  430.2 9.1 %reshape.674 = bf16[1867104]{0:T(1024)(128)(2,1)} reshape(bf16[2,933552]{1,0:T(2,128)(2,1)} %get-tuple-element.50) | data formatting | bytes 7468416
  439.3 13.3 %reshape.607 = bf16[2,2161,432]{2,1,0:T(8,128)(2,1)} reshape(bf16[1867104]{0:T(1024)(128)(2,1)} %reshape.674) | data formatting | bytes 7468416 | tf_op jit(solution)/shard_map/reshape | solution.py:71
  452.6 9.1 %reshape.672 = bf16[1867104]{0:T(1024)(128)(2,1)} reshape(bf16[2,933552]{1,0:T(2,128)(2,1)} %get-tuple-element.51) | data formatting | bytes 7468416
  461.7 13.1 %reshape.608 = bf16[2,2161,432]{2,1,0:T(8,128)(2,1)} reshape(bf16[1867104]{0:T(1024)(128)(2,1)} %reshape.672) | data formatting | bytes 7468416 | tf_op jit(solution)/shard_map/reshape | solution.py:71
  474.8 9.1 %reshape.670 = bf16[1867104]{0:T(1024)(128)(2,1)} reshape(bf16[2,933552]{1,0:T(2,128)(2,1)} %get-tuple-element.53) | data formatting | bytes 7468416
  483.8 13.1 %reshape.609 = bf16[2,2161,432]{2,1,0:T(8,128)(2,1)} reshape(bf16[1867104]{0:T(1024)(128)(2,1)} %reshape.670) | data formatting | bytes 7468416 | tf_op jit(solution)/shard_map/reshape | solution.py:71
  496.9 9.4 %reshape.668 = bf16[1867104]{0:T(1024)(128)(2,1)} reshape(bf16[2,933552]{1,0:T(2,128)(2,1)} %get-tuple-element.52) | data formatting | bytes 7468416
  506.4 12.9 %reshape.610 = bf16[2,2161,432]{2,1,0:T(8,128)(2,1)} reshape(bf16[1867104]{0:T(1024)(128)(2,1)} %reshape.668) | data formatting | bytes 7468416 | tf_op jit(solution)/shard_map/reshape | solution.py:71
  519.3 1.5 dynamic-update-slice.1
  520.8 1.5 dynamic-update-slice.2
  522.3 7.5 %slice.418 = bf16[2,933552]{1,0:T(2,128)(2,1)} slice(bf16[2,939696]{1,0:T(2,128)(2,1)} %dynamic-update-slice.2), slice={[0:2], [5632:939184]} | slice | bytes 7468416 | tf_op jit(solution)/shard_map/slice | solution.py:71
  529.9 9.0 %reshape.666 = bf16[1867104]{0:T(1024)(128)(2,1)} reshape(bf16[2,933552]{1,0:T(2,128)(2,1)} %slice.418) | data formatting | bytes 7468416
  538.9 13.1 %reshape.611 = bf16[2,2161,432]{2,1,0:T(8,128)(2,1)} reshape(bf16[1867104]{0:T(1024)(128)(2,1)} %reshape.666) | data formatting | bytes 7468416 | tf_op jit(solution)/shard_map/reshape | solution.py:71
  552.0 14.9 %fusion.79 = (bf16[2,2160,432]{2,1,0:T(8,128)(2,1)}, bf16[2,2160,432]{2,1,0:T(8,128)(2,1)}, bf16[2,2160,432]{2,1,0:T(8,128)(2,1)}, bf16[2,2160,432]{2,1,0:T(8,128)(2,1)}) fusion(bf16[2,2161,432]{2,1,0:T(8,128)(2,1)} %reshape.600, bf16[2,2161,432]{2,1,0:T(8,128)(2,1)} %reshape.601), kind=kLoop, calls=%fused_computation.177 | loop fusion | bytes 29859840 | tf_op jit(solution)/shard_map/slice | solution.py:75
  567.0 12.9 %fusion.81 = (bf16[2,2160,432]{2,1,0:T(8,128)(2,1)}, bf16[2,2160,432]{2,1,0:T(8,128)(2,1)}, bf16[2,2160,432]{2,1,0:T(8,128)(2,1)}, bf16[2,2160,432]{2,1,0:T(8,128)(2,1)}) fusion(bf16[2,2161,432]{2,1,0:T(8,128)(2,1)S(1)} %bitcast.105, bf16[2,2161,432]{2,1,0:T(8,128)(2,1)} %reshape.603), kind=kLoop, calls=%fused_computation.179 | loop fusion | bytes 29859840 | tf_op jit(solution)/shard_map/slice | solution.py:75
  580.0 8.5 %fusion.83 = (bf16[2,2160,432]{2,1,0:T(8,128)(2,1)}, bf16[2,2160,432]{2,1,0:T(8,128)(2,1)}, bf16[2,2160,432]{2,1,0:T(8,128)(2,1)}, bf16[2,2160,432]{2,1,0:T(8,128)(2,1)}) fusion(bf16[2,2161,432]{2,1,0:T(8,128)(2,1)S(1)} %bitcast.107, bf16[2,2161,432]{2,1,0:T(8,128)(2,1)S(1)} %bitcast.109), kind=kLoop, calls=%fused_computation.181 | loop fusion | bytes 29859840 | tf_op jit(solution)/shard_map/slice | solution.py:75
  588.6 8.5 %fusion.85 = (bf16[2,2160,432]{2,1,0:T(8,128)(2,1)}, bf16[2,2160,432]{2,1,0:T(8,128)(2,1)}, bf16[2,2160,432]{2,1,0:T(8,128)(2,1)}, bf16[2,2160,432]{2,1,0:T(8,128)(2,1)}) fusion(bf16[2,2161,432]{2,1,0:T(8,128)(2,1)S(1)} %bitcast.111, bf16[2,2161,432]{2,1,0:T(8,128)(2,1)S(1)} %bitcast.115), kind=kLoop, calls=%fused_computation.183 | loop fusion | bytes 29859840 | tf_op jit(solution)/shard_map/slice | solution.py:75
  597.1 7.0 fusion.87
  604.2 7.0 fusion.89
  611.2 32.1 %bitcast_convert_fusion = bf16[2,512,2160]{1,2,0:T(8,128)(2,1)} fusion(bf16[2,2160,432]{2,1,0:T(8,128)(2,1)} %get-tuple-element.100, bf16[2,2160,432]{2,1,0:T(8,128)(2,1)} %get-tuple-element.101, bf16[2,2160,432]{2,1,0:T(8,128)(2,1)} %get-tuple-element.40, bf16[2,2160,432]{2,1,0:T(8,128)(2,1)} %get-tuple-element.39, ...), kind=kOutput, calls=%fused_computation.3 | convolution fusion | flops 4692361216 | bytes 96124928 | tf_op jit(solution)/shard_map/pqkn,qsn->pks/dot_general | solution.py:147
  643.3 12.2 %copy.70 = bf16[2,512,2160]{2,0,1:T(2,128)(2,1)} copy(bf16[2,512,2160]{1,2,0:T(8,128)(2,1)} %bitcast_convert_fusion) | data formatting | bytes 8847360 | tf_op jit(solution)/shard_map/convert_element_type | solution.py:149
  655.6 3.4 gather_fusion
  659.1 0.8 copy.72
  660.0 8.4 %all-to-all-start = ((bf16[2,3,8,2160]{3,0,1,2:T(2,128)(2,1)}), bf16[2,3,8,2160]{3,0,1,2:T(2,128)(2,1)S(1)}, u32[]{:S(2)}, u32[]{:S(2)}) async-start(bf16[2,3,8,2160]{3,0,1,2:T(2,128)(2,1)} %copy.72), calls=%async_computation | async-start | bytes 417792 | tf_op jit(solution)/shard_map/all_to_all | solution.py:170
  668.4 1.2 fusion.72
  670.4 5.8 all-to-all-done
  677.7 0.8 fusion.23
  678.5 1.9 copy.89
  680.4 7.7 %gather_fusion.1 = f32[3172,3]{1,0:T(8,128)} fusion(f32[3,6912]{0,1:T(8,128)S(1)} %bitcast.125, s32[4096]{0:T(1024)} %pad_clamp_fusion.1), kind=kCustom, calls=%fused_computation.clone | custom fusion | bytes 88816 | tf_op jit(solution)/shard_map/jit(_take)/gather | solution.py:116
  688.1 2.5 copy.82
  690.7 7.0 gather_fusion.2
  697.7 1.9 copy.83
  699.6 0.9 pad_maximum_fusion.13
  700.5 31.8 %all_gather.3 = f32[2,24,1,3172]{3,0,2,1:T(2,128)S(1)} all-gather(f32[2,3,1,3172]{3,0,2,1:T(2,128)S(1)} %pad_maximum_fusion.13), channel_id=1, replica_groups=mesh['groups'=2,'tm'=4,'zoom'=2,'pol'=2] {'tm','zoom'}, dimensions={1}, use_global_device_ids=true | all-gather | bytes 685152 | tf_op jit(solution)/shard_map/all_gather | solution.py:175
  732.2 0.9 convolution_bitcast_fusion
  733.3 1.3 collective-permute-start.1
  734.6 1.3 collective-permute-start.2
  735.9 0.8 broadcast_reduce_fusion
  736.8 3.2 collective-permute-done.2
  (130 shorter events, 12.0 us)
Async XLA Ops:
  0.8 20.4 %copy-start.10 = (f32[12,512]{1,0:T(8,128)S(1)}, f32[12,512]{1,0:T(8,128)}, u32[]{:S(2)}) copy-start(f32[12,512]{1,0:T(8,128)} %param.10) | copy-start | bytes 73732
  0.8 20.4 %copy-start.18 = (s32[2]{0:T(128)S(1)}, s32[2]{0:T(128)}, u32[]{:S(2)}) copy-start(s32[2]{0:T(128)} %param.13) | copy-start | bytes 28
  0.8 21.4 %copy-start.16 = (s32[2]{0:T(128)S(1)}, s32[2]{0:T(128)}, u32[]{:S(2)}) copy-start(s32[2]{0:T(128)} %param.12) | copy-start | bytes 28
  0.8 22.4 %copy-start.12 = (s32[3172]{0:T(1024)S(1)}, s32[3172]{0:T(1024)}, u32[]{:S(2)}) copy-start(s32[3172]{0:T(1024)} %constant.143) | copy-start | bytes 38068
  0.8 23.0 %copy-start.11 = (s32[3172]{0:T(1024)S(1)}, s32[3172]{0:T(1024)}, u32[]{:S(2)}) copy-start(s32[3172]{0:T(1024)} %constant.144) | copy-start | bytes 38068
  0.8 29.7 %collective-permute-start = (bf16[2,5712]{1,0:T(2,128)(2,1)S(1)}, bf16[2,5712]{1,0:T(2,128)(2,1)S(1)}, u32[]{:S(2)}, u32[]{:S(2)}) collective-permute-start(bf16[2,5712]{1,0:T(2,128)(2,1)S(1)} %slice.375), channel_id=1, source_target_pairs={{2,0},{4,2},{6,4},{8,6},{10,8},{12,10},{14,12},{3,1},{5,3},{7,5},{... | collective-permute-start | bytes 68552 | tf_op jit(solution)/shard_map/ppermute | solution.py:21
  25.7 1.9 copy-start.13
  538.9 28.0 %slice-start = ((s8[4440064]{0:T(1024)(128)(4,1)}), s8[245760]{0:T(1024)(128)(4,1)S(1)}, s32[]{:S(2)}) async-start(s8[4440064]{0:T(1024)(128)(4,1)} %bitcast.104), calls=%async_computation.1 | async-start | bytes 491520
  552.0 14.9 %slice-start.1 = ((s8[4440064]{0:T(1024)(128)(4,1)}), s8[4194304]{0:T(1024)(128)(4,1)S(1)}, s32[]{:S(2)}) async-start(s8[4440064]{0:T(1024)(128)(4,1)} %bitcast.104), calls=%async_computation.2 | async-start | bytes 8388608
  552.0 27.9 %slice-start.2 = ((s8[4440064]{0:T(1024)(128)(4,1)}), s8[4194304]{0:T(1024)(128)(4,1)S(1)}, s32[]{:S(2)}) async-start(s8[4440064]{0:T(1024)(128)(4,1)} %bitcast.106), calls=%async_computation.3 | async-start | bytes 8388608
  552.0 27.9 %slice-start.4 = ((s8[4440064]{0:T(1024)(128)(4,1)}), s8[4194304]{0:T(1024)(128)(4,1)S(1)}, s32[]{:S(2)}) async-start(s8[4440064]{0:T(1024)(128)(4,1)} %bitcast.108), calls=%async_computation.5 | async-start | bytes 8388608
  567.0 13.0 %slice-start.3 = ((s8[4440064]{0:T(1024)(128)(4,1)}), s8[245760]{0:T(1024)(128)(4,1)S(1)}, s32[]{:S(2)}) async-start(s8[4440064]{0:T(1024)(128)(4,1)} %bitcast.106), calls=%async_computation.4 | async-start | bytes 491520
  567.0 13.0 %slice-start.5 = ((s8[4440064]{0:T(1024)(128)(4,1)}), s8[245760]{0:T(1024)(128)(4,1)S(1)}, s32[]{:S(2)}) async-start(s8[4440064]{0:T(1024)(128)(4,1)} %bitcast.108), calls=%async_computation.6 | async-start | bytes 491520
  567.0 21.5 %slice-start.6 = ((s8[4440064]{0:T(1024)(128)(4,1)}), s8[4194304]{0:T(1024)(128)(4,1)S(1)}, s32[]{:S(2)}) async-start(s8[4440064]{0:T(1024)(128)(4,1)} %bitcast.110), calls=%async_computation.7 | async-start | bytes 8388608
  567.0 21.5 %slice-start.10 = ((s8[4440064]{0:T(1024)(128)(4,1)}), s8[4194304]{0:T(1024)(128)(4,1)S(1)}, s32[]{:S(2)}) async-start(s8[4440064]{0:T(1024)(128)(4,1)} %bitcast.114), calls=%async_computation.11 | async-start | bytes 8388608
  580.0 8.5 %slice-start.7 = ((s8[4440064]{0:T(1024)(128)(4,1)}), s8[245760]{0:T(1024)(128)(4,1)S(1)}, s32[]{:S(2)}) async-start(s8[4440064]{0:T(1024)(128)(4,1)} %bitcast.110), calls=%async_computation.8 | async-start | bytes 491520
  580.0 8.5 %slice-start.11 = ((s8[4440064]{0:T(1024)(128)(4,1)}), s8[245760]{0:T(1024)(128)(4,1)S(1)}, s32[]{:S(2)}) async-start(s8[4440064]{0:T(1024)(128)(4,1)} %bitcast.114), calls=%async_computation.12 | async-start | bytes 491520
  580.0 17.1 %slice-start.8 = ((s8[4440064]{0:T(1024)(128)(4,1)}), s8[4194304]{0:T(1024)(128)(4,1)S(1)}, s32[]{:S(2)}) async-start(s8[4440064]{0:T(1024)(128)(4,1)} %bitcast.112), calls=%async_computation.9 | async-start | bytes 8388608
  580.0 17.1 %slice-start.14 = ((s8[4440064]{0:T(1024)(128)(4,1)}), s8[4194304]{0:T(1024)(128)(4,1)S(1)}, s32[]{:S(2)}) async-start(s8[4440064]{0:T(1024)(128)(4,1)} %bitcast.118), calls=%async_computation.15 | async-start | bytes 8388608
  588.5 8.5 %slice-start.9 = ((s8[4440064]{0:T(1024)(128)(4,1)}), s8[245760]{0:T(1024)(128)(4,1)S(1)}, s32[]{:S(2)}) async-start(s8[4440064]{0:T(1024)(128)(4,1)} %bitcast.112), calls=%async_computation.10 | async-start | bytes 491520
  588.5 8.5 %slice-start.15 = ((s8[4440064]{0:T(1024)(128)(4,1)}), s8[245760]{0:T(1024)(128)(4,1)S(1)}, s32[]{:S(2)}) async-start(s8[4440064]{0:T(1024)(128)(4,1)} %bitcast.118), calls=%async_computation.16 | async-start | bytes 491520
  588.5 15.6 %slice-start.12 = ((s8[4440064]{0:T(1024)(128)(4,1)}), s8[4194304]{0:T(1024)(128)(4,1)S(1)}, s32[]{:S(2)}) async-start(s8[4440064]{0:T(1024)(128)(4,1)} %bitcast.116), calls=%async_computation.13 | async-start | bytes 8388608
  588.5 15.6 %slice-start.16 = ((s8[4440064]{0:T(1024)(128)(4,1)}), s8[4194304]{0:T(1024)(128)(4,1)S(1)}, s32[]{:S(2)}) async-start(s8[4440064]{0:T(1024)(128)(4,1)} %bitcast.120), calls=%async_computation.17 | async-start | bytes 8388608
  597.1 7.1 slice-start.13
  597.1 7.1 slice-start.17
  604.2 7.0 copy-start
  643.3 15.7 %copy-start.15 = (pred[3,8]{1,0:T(4,128)(4,1)S(1)}, pred[3,8]{1,0:T(4,128)(4,1)}, u32[]{:S(2)}) copy-start(pred[3,8]{1,0:T(4,128)(4,1)} %copy.68) | copy-start | bytes 76
  643.3 26.3 %copy-start.6 = (f32[5,3456]{1,0:T(8,128)S(1)}, f32[5,3456]{1,0:T(8,128)}, u32[]{:S(2)}) copy-start(f32[5,3456]{1,0:T(8,128)} %param.11) | copy-start | bytes 207364
  643.3 26.4 %copy-start.14 = (f32[5]{0:T(128)S(1)}, f32[5]{0:T(128)}, u32[]{:S(2)}) copy-start(f32[5]{0:T(128)} %get-tuple-element.108) | copy-start | bytes 64
  643.3 26.4 %copy-start.17 = (f32[128]{0:T(128)S(1)}, f32[128]{0:T(128)}, u32[]{:S(2)}) copy-start(f32[128]{0:T(128)} %add_multiply_fusion) | copy-start | bytes 1540
  643.3 34.1 %copy-start.1 = (bf16[1,2,27,27]{3,2,1,0:T(8,128)(2,1)S(1)}, bf16[1,2,27,27]{3,2,1,0:T(8,128)(2,1)}, u32[]{:S(2)}) copy-start(bf16[1,2,27,27]{3,2,1,0:T(8,128)(2,1)} %get-tuple-element.81) | copy-start | bytes 8752
  643.3 34.1 %copy-start.2 = (bf16[1,2,27,27]{3,2,1,0:T(8,128)(2,1)S(1)}, bf16[1,2,27,27]{3,2,1,0:T(8,128)(2,1)}, u32[]{:S(2)}) copy-start(bf16[1,2,27,27]{3,2,1,0:T(8,128)(2,1)} %get-tuple-element.82) | copy-start | bytes 8752
  655.6 22.0 %copy-start.3 = (f32[27,128]{1,0:T(8,128)S(1)}, f32[27,128]{1,0:T(8,128)}, u32[]{:S(2)}) copy-start(f32[27,128]{1,0:T(8,128)} %get-tuple-element.104) | copy-start | bytes 41476
  655.6 22.0 %copy-start.4 = (f32[27,128]{1,0:T(8,128)S(1)}, f32[27,128]{1,0:T(8,128)}, u32[]{:S(2)}) copy-start(f32[27,128]{1,0:T(8,128)} %get-tuple-element.105) | copy-start | bytes 41476
  655.6 22.1 %copy-start.7 = (bf16[128,128]{1,0:T(8,128)(2,1)S(1)}, bf16[128,128]{1,0:T(8,128)(2,1)}, u32[]{:S(2)}) copy-start(bf16[128,128]{1,0:T(8,128)(2,1)} %get-tuple-element.106) | copy-start | bytes 98308
  655.6 22.1 %copy-start.8 = (bf16[128,128]{1,0:T(8,128)(2,1)S(1)}, bf16[128,128]{1,0:T(8,128)(2,1)}, u32[]{:S(2)}) copy-start(bf16[128,128]{1,0:T(8,128)(2,1)} %get-tuple-element.107) | copy-start | bytes 98308
  655.6 22.1 %copy-start.9 = (bf16[128,128]{1,0:T(8,128)(2,1)S(1)}, bf16[128,128]{1,0:T(8,128)(2,1)}, u32[]{:S(2)}) copy-start(bf16[128,128]{1,0:T(8,128)(2,1)} %fusion.54) | copy-start | bytes 98308
  660.0 16.3 %all-to-all-start = ((bf16[2,3,8,2160]{3,0,1,2:T(2,128)(2,1)}), bf16[2,3,8,2160]{3,0,1,2:T(2,128)(2,1)S(1)}, u32[]{:S(2)}, u32[]{:S(2)}) async-start(bf16[2,3,8,2160]{3,0,1,2:T(2,128)(2,1)} %copy.72), calls=%async_computation | async-start | bytes 417792 | tf_op jit(solution)/shard_map/all_to_all | solution.py:170
  676.3 14.4 %copy-start.5 = (s32[4096]{0:T(1024)S(1)}, s32[4096]{0:T(1024)}, u32[]{:S(2)}) copy-start(s32[4096]{0:T(1024)} %pad_clamp_fusion) | copy-start | bytes 49156
  733.3 3.5 collective-permute-start.1
  734.6 5.5 collective-permute-start.2
where the time goes:
time: 750 us; the launch traced here: 742 us
  local copies, waits for them, and re-layouts  387 us (52%)
  other arithmetic  266 us (35%)
  matrix products  34 us (5%)
  blocking collectives  31.8 us (4%)
  starting transfers between devices  12.4 us (2%)
  waiting for transfers between devices  9.08 us (1%)
    concatenate x2, other arithmetic, on_device(): jnp.concatenate([signal, following, jnp.zeros((2, pieces * HOP), jnp.bflo...  243 us
    reshape x12, local copies, waits for them, and re-layouts, frame_view(): segment[:, :(spectra + pieces - 1) * hop_len]  157 us
    unnamed x88, local copies, waits for them, and re-layouts  120 us
    slice x6, local copies, waits for them, and re-layouts, frame_view(): framed[:, offset:offset + spectra]  58.8 us
    dot_general x1, matrix products, on_device(): jnp.einsum('pqkn,qsn->pks', rotation_block(chan_len), weighted, preferred...  32.1 us
    all_gather x1, blocking collectives, on_device(): piece = lax.all_gather(computed, ('tm', 'zoom'), axis=1, tiled=True)  31.8 us
  transfers between devices with their start and end apart: 4, of which 2 were waited for; matrix products, arithmetic and copies ran while one was open for 4% of the time, Pallas kernels for 0%

commit v1 on v0

v1 whole, which is shorter than its diff:
```python
import functools
import math

import jax
import jax.numpy as jnp
import numpy as np
from jax import lax
from jax.experimental import pallas as pl
from jax.experimental.pallas import tpu as pltpu
from jax.sharding import PartitionSpec as P

HOP = 432
FA = 27
FB = 128
KEEP = 2916
EDGE = 128
CH_DEV = 5


def shifted(value, axis, steps):
    count = lax.axis_size(axis)
    initial, last = (max(0, -steps), min(count, count - steps))
    return lax.ppermute(value, axis, [(source, source + steps) for source in range(initial, last)])


def angle_table(rows, cols, length):
    product = (
        jnp.arange(rows, dtype=jnp.int32)[:, None]
        * jnp.arange(cols, dtype=jnp.int32)[None, :]
        % length
    )
    return product.astype(jnp.float32) * (2.0 * math.pi / length)


def rotation_block(length):
    angles = angle_table(length, length, length)
    cosine_tab = jnp.cos(angles).astype(jnp.bfloat16)
    sine_tab = jnp.sin(angles).astype(jnp.bfloat16)
    return jnp.stack([jnp.stack([cosine_tab, sine_tab]), jnp.stack([-sine_tab, cosine_tab])])


def joined_table(length):
    angles = angle_table(length, length, length)
    cosine_tab = jnp.cos(angles).astype(jnp.bfloat16)
    sine_tab = jnp.sin(angles).astype(jnp.bfloat16)
    top_rows = jnp.concatenate([cosine_tab, -sine_tab], axis=1)
    bottom_rows = jnp.concatenate([sine_tab, cosine_tab], axis=1)
    return jnp.concatenate([top_rows, bottom_rows], axis=0)


def frame_view(segment, spectra, chan_len, hop_len):
    pieces = -(-chan_len // hop_len)
    framed = segment[:, : (spectra + pieces - 1) * hop_len].reshape(
        segment.shape[0], spectra + pieces - 1, hop_len
    )
    joined = jnp.concatenate(
        [framed[:, offset : offset + spectra] for offset in range(pieces)], axis=2
    )
    return joined[:, :, :chan_len]


def weighted_frames(signal, taps, spectra, hop_len):
    chan_len = taps.shape[1]
    running = jnp.zeros((2, spectra, chan_len), jnp.float32)
    for tap_index in range(taps.shape[0]):
        frames = frame_view(signal[:, tap_index * chan_len :], spectra, chan_len, hop_len)
        running = running + taps[tap_index][None, None, :] * frames.astype(jnp.float32)
    return running.astype(jnp.bfloat16)


def fine_spectra(series, section2_taps, radix_a, radix_b, keep_len, edge_len):
    tap_count, fine_len = section2_taps.shape
    items = series.shape[1]
    row_count = series.shape[2] // fine_len
    spectra = row_count - tap_count + 1
    row_blocks = series.reshape(2, items, row_count, fine_len)
    running = jnp.zeros((2, items, spectra, fine_len), jnp.float32)
    for tap_index in range(tap_count):
        running = running + section2_taps[tap_index] * row_blocks[
            :, :, tap_index : tap_index + spectra
        ].astype(jnp.float32)
    weighted = running.astype(jnp.bfloat16).reshape(2, items, spectra, radix_a, radix_b)
    partial_value = jnp.einsum(
        "pqkm,qcfmb->pcfkb", rotation_block(radix_a), weighted, preferred_element_type=jnp.float32
    )
    angles = angle_table(radix_a, radix_b, fine_len)
    cosine_tab = jnp.cos(angles)
    sine_tab = jnp.sin(angles)
    real_part = partial_value[0] * cosine_tab + partial_value[1] * sine_tab
    imag_part = partial_value[1] * cosine_tab - partial_value[0] * sine_tab
    twiddled = jnp.concatenate([real_part, imag_part], axis=-1).astype(jnp.bfloat16)
    table = joined_table(radix_b).reshape(2 * radix_b, 2, radix_b)
    spectrum = jnp.einsum(
        "cfkm,mpq->pcfqk", twiddled, table, preferred_element_type=jnp.float32
    ).reshape(2, items, spectra, fine_len)
    first = (-(keep_len // 2) - edge_len) % fine_len
    rest = keep_len + 2 * edge_len - (fine_len - first)
    return jnp.concatenate([spectrum[..., first:], spectrum[..., :rest]], axis=-1)


def stitch_bands(extended, upper_rim, lower_rim, slot_ids, band_width, keep_len, edge_len):
    centre = extended[..., edge_len : edge_len + keep_len]
    live = (slot_ids < band_width).astype(jnp.float32)[None, :, None, None]
    upper_ok = (slot_ids + 1 < band_width).astype(jnp.float32)[None, :, None, None]
    lower_ok = ((slot_ids >= 1) & (slot_ids < band_width)).astype(jnp.float32)[None, :, None, None]
    ramp = (jnp.arange(edge_len, dtype=jnp.float32) + 0.5) / (2.0 * edge_len)
    upper_weight = ramp * upper_ok
    lower_weight = ramp[::-1] * lower_ok
    low_part = centre[..., :edge_len] * (1.0 - lower_weight) + lower_rim * lower_weight
    high_part = centre[..., keep_len - edge_len :] * (1.0 - upper_weight) + upper_rim * upper_weight
    joined = jnp.concatenate(
        [low_part, centre[..., edge_len : keep_len - edge_len], high_part], axis=-1
    )
    return joined * live


GROUP = 8
CHUNK = 1152


def bank_kernel(turns, halves, per_row, x_ref, taps_ref, rot_ref, out_ref, bank, total):
    step = pl.program_id(0)
    half = rot_ref.shape[1] // 2
    chans = half // GROUP
    rot_len = rot_ref.shape[0]
    piece = 128
    lane = lax.broadcasted_iota(jnp.int32, (piece, half), 1) // chans

    @pl.when(step == 0)
    def _():
        total[...] = jnp.zeros_like(total)

    @pl.loop(0, CHUNK // piece)
    def _(part):
        row = pl.multiple_of(part * piece, piece)
        turn = pl.multiple_of((step * CHUNK + row) % rot_len, piece)
        taps = taps_ref[pl.ds(row, piece), :]
        wide = jnp.broadcast_to(taps[:, 0:1], (piece, half))
        for phase in range(1, GROUP):
            wide = jnp.where(lane == phase, taps[:, phase : phase + 1], wide)
        for tab in range(2):
            cols = pl.ds(tab * half, half)
            bank[pl.ds(row, piece), cols] = (
                wide * rot_ref[pl.ds(turn, piece), cols]
            ).astype(jnp.bfloat16)

    shift = step // per_row
    total[shift] += jnp.dot(x_ref[...], bank[...], preferred_element_type=jnp.float32)

    @pl.when(step == pl.num_programs(0) - 1)
    def _():
        rows = out_ref.shape[1]
        real = jnp.zeros((rows, half), jnp.float32)
        imag = jnp.zeros((rows, half), jnp.float32)
        for shift in range(turns):
            upper, lower = pl.ds(shift, rows), pl.ds(halves + shift, rows)
            real += total[shift, upper, :half] + total[shift, lower, half:]
            imag += total[shift, lower, :half] - total[shift, upper, half:]
        out_ref[0] = real.astype(jnp.bfloat16)
        out_ref[1] = imag.astype(jnp.bfloat16)


def slot_bank(signal, taps, channels, spectra):
    tap_count, chan_len = taps.shape
    row_len = GROUP * HOP
    rows = -(-spectra // GROUP)
    reach = (GROUP - 1) * HOP + tap_count * chan_len
    steps = -(-reach // CHUNK)
    per_row = row_len // CHUNK
    turns = -(-steps // per_row)
    halves = -(-(rows + turns - 1) // 16) * 16
    keep = -(-rows // 16) * 16
    if keep + turns - 1 > halves:
        halves += 16
    fill = halves * row_len - signal.shape[1]
    data = jnp.pad(signal, ((0, 0), (0, fill))).reshape(2 * halves, row_len)
    flat = taps.reshape(-1)
    spread = jnp.stack(
        [
            jnp.pad(flat, (phase * HOP, steps * CHUNK - flat.shape[0] - phase * HOP))
            for phase in range(GROUP)
        ],
        axis=1,
    )
    chans = channels.shape[0]
    places = (
        jnp.arange(chan_len, dtype=jnp.int32)[:, None]
        - HOP * jnp.arange(GROUP, dtype=jnp.int32)[None, :]
    ) % chan_len
    places = jnp.repeat(places, chans, axis=1)
    turns_of = places * jnp.tile(channels, GROUP)[None, :] % chan_len
    angles = turns_of.astype(jnp.float32) * (2.0 * math.pi / chan_len)
    rot = jnp.concatenate([jnp.cos(angles), jnp.sin(angles)], axis=1)
    rot = rot.astype(jnp.bfloat16).astype(jnp.float32)
    half = GROUP * chans
    out = pl.pallas_call(
        functools.partial(bank_kernel, turns, halves, per_row),
        grid=(steps,),
        in_specs=[
            pl.BlockSpec((2 * halves, CHUNK), lambda i: (0, i % per_row)),
            pl.BlockSpec((CHUNK, GROUP), lambda i: (i, 0)),
            pl.BlockSpec((chan_len, 2 * half), lambda i: (0, 0)),
        ],
        out_specs=pl.BlockSpec((2, keep, half), lambda i: (0, 0, 0)),
        out_shape=jax.ShapeDtypeStruct((2, keep, half), jnp.bfloat16),
        scratch_shapes=[
            pltpu.VMEM((CHUNK, 2 * half), jnp.bfloat16),
            pltpu.VMEM((turns, 2 * halves, 2 * half), jnp.float32),
        ],
        name="slot_bank",
    )(data, spread, rot)
    out = out[:, :rows].reshape(2, rows, GROUP, chans)
    return jnp.transpose(out, (0, 3, 1, 2)).reshape(2, chans, rows * GROUP)[:, :, :spectra]


def on_device(voltages, section1_taps, section2_taps, band_starts, band_widths):
    signal = voltages[0]
    tap_count, chan_len = section1_taps.shape
    spectra = signal.shape[1] // HOP
    rim_len = tap_count * chan_len - HOP
    tm_count = lax.axis_size("tm")
    zoom_count = lax.axis_size("zoom")
    device_count = tm_count * zoom_count
    slot_count = tm_count * CH_DEV
    following = shifted(signal[:, :rim_len], ("tm", "zoom"), -1)
    offsets = np.arange(-1, CH_DEV + 1)
    slots = np.clip(np.arange(tm_count)[:, None] * CH_DEV + offsets[None, :], 0, slot_count - 1)
    wanted = slots[:, None, :] + slot_count * np.arange(zoom_count)[None, :, None]
    wanted = wanted.reshape(device_count, CH_DEV + 2)
    all_slots = jnp.arange(slot_count, dtype=jnp.int32)
    channels = ((band_starts[:, None] + all_slots[None, :]) % chan_len).reshape(-1)
    if channels.shape[0] <= 48:
        joined = jnp.concatenate([signal, following], axis=1)
        width = -(-channels.shape[0] // 16) * 16
        padded = jnp.pad(channels, (0, width - channels.shape[0]))
        coarse = slot_bank(joined, section1_taps, padded, spectra)
        packed = jnp.stack(
            [
                jnp.stack([coarse[:, int(index)] for index in wanted[:, place]], axis=1)
                for place in range(CH_DEV + 2)
            ],
            axis=1,
        )
    else:
        pieces = -(-chan_len // HOP)
        padded = jnp.concatenate(
            [signal, following, jnp.zeros((2, pieces * HOP), jnp.bfloat16)], axis=1
        )
        weighted = weighted_frames(padded, section1_taps, spectra, HOP)
        coarse = jnp.einsum(
            "pqkn,qsn->pks", rotation_block(chan_len), weighted, preferred_element_type=jnp.float32
        ).astype(jnp.bfloat16)
        order = channels[wanted.T.reshape(-1)]
        packed = jnp.take(coarse, order, axis=1).reshape(2, CH_DEV + 2, device_count, spectra)
    received = lax.all_to_all(packed, ("tm", "zoom"), split_axis=2, concat_axis=2, tiled=True)
    series = received.reshape(2, CH_DEV + 2, -1)
    spans = fine_spectra(series, section2_taps, FA, FB, KEEP, EDGE)
    slot_ids = lax.axis_index("tm") * CH_DEV + jnp.arange(CH_DEV, dtype=jnp.int32)
    band_ids = jnp.arange(band_widths.shape[0], dtype=jnp.int32)
    band_width = jnp.sum(jnp.where(band_ids == lax.axis_index("zoom"), band_widths, 0))
    upper_rim = spans[:, 2:, :, :EDGE]
    lower_rim = spans[:, :CH_DEV, :, KEEP + EDGE :]
    extended = spans[:, 1 : CH_DEV + 1]
    stitched = stitch_bands(extended, upper_rim, lower_rim, slot_ids, band_width, KEEP, EDGE)
    fine_count = stitched.shape[2]
    result = jnp.transpose(stitched, (0, 2, 1, 3)).reshape(2, fine_count, CH_DEV * KEEP)
    return result[None, None]


def solution(mesh):
    placed = (P("pol", "groups", ("tm", "zoom")), P(), P(), P("groups"), P("groups"))
    return jax.shard_map(
        on_device,
        mesh=mesh,
        in_specs=placed,
        out_specs=P("pol", "zoom", "groups", None, "tm"),
        check_vma=False,
    )
```

time: 750 us -> 208 us (0.28)
  local copies, waits for them, and re-layouts: 387 us -> 122 us
  other arithmetic: 266 us -> 30.2 us
  matrix products: 34 us -> 0.43 us
  blocking collectives: 31.8 us -> 0 us
  Pallas kernels: 0 us -> 30 us
    concatenate x3, other arithmetic: 243 us -> 20.8 us  [the longest x1 20.6 us: on_device(): joined = jnp.concatenate([signal, following], axis=1)]
    reshape x14 -> x4, local copies, waits for them, and re-layouts: 159 us -> 8.36 us  [the longest x1 6.63 us: slot_bank(): data = jnp.pad(signal, ((0, 0), (0, fill))).reshape(2 * halves, row_len)]
    unnamed x88 -> x44, local copies, waits for them, and re-layouts: 120 us -> 13.3 us
    another operation x4 -> x13, local copies, waits for them, and re-layouts: 4.63 us -> 71.6 us  [the longest x7 59.8 us: on_device(): jnp.stack([coarse[:, int(index)] for index in wanted[:, place]], axis=1)]
    slice x10 -> x5, local copies, waits for them, and re-layouts: 66.4 us -> 22.6 us  [the longest x3 21.1 us: on_device(): coarse[:, int(index)]]
    dot_general x3 -> x1, matrix products: 33.9 us -> 0.21 us  [fine_spectra(): jnp.einsum('cfkm,mpq->pcfqk', twiddled, table, preferred_element_type=jnp...]
    all_gather x1 -> x0, blocking collectives: 31.8 us -> none  [on_device(): piece = lax.all_gather(computed, ('tm', 'zoom'), axis=1, tiled=True)]
    pallas_call x0 -> x1, Pallas kernels: none -> 30 us  [slot_bank(): pl.pallas_call(functools.partial(bank_kernel, turns, halves, per_row), gr...]
  transfers between devices with their start and end apart: 4 -> 2, of which waited for: 2 -> 1; matrix products, arithmetic and copies ran while one was open for 4% -> 7% of each run, Pallas kernels for 0% -> 0%
where the time goes in v1:
time: 208 us; the launch traced here: 205 us
  local copies, waits for them, and re-layouts  122 us (59%)
  other arithmetic  30.2 us (15%)
  Pallas kernels  30 us (14%)
  waiting for transfers between devices  12.9 us (6%)
  starting transfers between devices  9.85 us (5%)
    another operation x7, local copies, waits for them, and re-layouts, on_device(): jnp.stack([coarse[:, int(index)] for index in wanted[:, place]], axis=1)  59.8 us
    pallas_call x1, Pallas kernels, slot_bank(): pl.pallas_call(functools.partial(bank_kernel, turns, halves, per_row), gr...  30 us
    slice x3, local copies, waits for them, and re-layouts, on_device(): coarse[:, int(index)]  21.1 us
    concatenate x1, other arithmetic, on_device(): joined = jnp.concatenate([signal, following], axis=1)  20.6 us
    unnamed x44, local copies, waits for them, and re-layouts  13.3 us
    all_to_all x1, waiting for transfers between devices, on_device(): lax.all_to_all(packed, ('tm', 'zoom'), split_axis=2, concat_axis=2, tiled...  12.9 us
    all_to_all x1, starting transfers between devices, on_device(): lax.all_to_all(packed, ('tm', 'zoom'), split_axis=2, concat_axis=2, tiled...  8.56 us
    another operation x2, local copies, waits for them, and re-layouts, on_device(): jnp.stack([jnp.stack([coarse[:, int(index)] for index in wanted[:, place]...  8.33 us
  transfers between devices with their start and end apart: 2, of which 1 were waited for; matrix products, arithmetic and copies ran while one was open for 7% of the time, Pallas kernels for 0%

profile of v1, /device:TPU:0, one launch (start us, length us, event | category | flops | bytes accessed | tf_op | source)
XLA Modules:
  0.0 205.4 jit_solution(8762407278704905631)
XLA Ops:
  0.0 0.8 slice.274
  0.8 1.3 collective-permute-start
  2.1 0.1 sine_convert_fusion.2
  2.3 0.7 fusion.24
  3.0 0.3 sine_convert_fusion.1
  3.3 0.3 fusion.33
  3.5 0.8 reshape.385
  4.3 0.1 fusion.46
  4.6 0.3 copy.213
  4.9 0.3 copy-done.17
  5.4 0.6 fusion.37
  6.1 0.6 compare_convert_fusion.1
  6.7 0.1 broadcast_reduce_fusion
  6.8 3.3 %cosine_convert_fusion = (bf16[512,384]{1,0:T(8,128)(2,1)S(1)}, bf16[512,384]{1,0:T(8,128)(2,1)S(1)}) fusion(s32[512,384]{1,0:T(8,128)S(1)} %copy.213, s32[384]{0:T(512)S(1)} %mul.397), kind=kLoop, calls=%fused_computation.21 | loop fusion | flops 3145728 | bytes 1574400 | tf_op jit(solution)/shard_map/convert.2
  10.1 1.3 maximum_convert_fusion.rot_ref
  11.4 0.6 maximum_bitcast_fusion.4
  12.0 0.6 compare_convert_fusion
  12.6 0.5 stack.99
  13.1 2.9 %copy.214.taps_ref = f32[9216,8]{1,0:T(8,128)} copy(f32[9216,8]{0,1:T(8,128)S(1)} %stack.99) | data formatting | bytes 589824 | tf_op jit(solution)/shard_map/stack | solution.py:178
  16.1 20.6 %fusion.2 = bf16[2,995328]{1,0:T(2,128)(2,1)} fusion(bf16[2,5712]{1,0:T(2,128)(2,1)S(1)} %collective-permute-done, bf16[2,933120]{1,0:T(2,128)(2,1)} %bitcast.86), kind=kLoop, calls=%fused_computation.3 | loop fusion | flops 13934592 | bytes 7736640 | tf_op jit(solution)/shard_map/concatenate | solution.py:233
  36.7 6.6 %reshape.384.x_ref = bf16[576,3456]{1,0:T(8,128)(2,1)} reshape(bf16[2,995328]{1,0:T(2,128)(2,1)} %fusion.2) | data formatting | bytes 7962624 | tf_op jit(solution)/shard_map/reshape | solution.py:176
  43.3 30.0 %slot_bank.1 = bf16[2,272,384]{2,1,0:T(8,128)(2,1)} custom-call(bf16[576,3456]{1,0:T(8,128)(2,1)} %reshape.384.x_ref, f32[9216,8]{1,0:T(8,128)} %copy.214.taps_ref, f32[512,768]{1,0:T(8,128)} %maximum_convert_fusion.rot_ref), custom_call_target="tpu_custom_call" | custom-call | tf_op jit(solution)/shard_map/slot_bank/pallas_call | solution.py:196
  73.3 1.3 copy.215
  74.6 0.9 copy.216
  75.6 9.2 %fusion.41 = (bf16[2,1,2160]{1,2,0:T(8,128)(2,1)S(1)}, bf16[2,1,2160]{1,2,0:T(8,128)(2,1)S(1)}, bf16[2,1,2160]{1,2,0:T(8,128)(2,1)}, bf16[2,1,2160]{1,2,0:T(8,12...) fusion(bf16[2,48,2160]{1,2,0:T(8,128)(2,1)S(1)} %bitcast.82), kind=kLoop, calls=%fused_computation.110 | loop fusion | bytes 328320 | tf_op jit(solution)/shard_map/slice | solution.py:239
  84.8 10.1 %fusion.42 = (bf16[2,1,2160]{1,2,0:T(8,128)(2,1)}, bf16[2,1,2160]{1,2,0:T(8,128)(2,1)}, bf16[2,1,2160]{1,2,0:T(8,128)(2,1)}, bf16[2,1,2160]{1,2,0:T(8,128)(2,1)}...) fusion(bf16[2,48,2160]{1,2,0:T(8,128)(2,1)S(1)} %bitcast.83), kind=kLoop, calls=%fused_computation.111 | loop fusion | bytes 328320 | tf_op jit(solution)/shard_map/slice | solution.py:239
  95.0 1.8 fusion.43
  96.7 8.6 %stack.112 = bf16[2,8,2160]{1,2,0:T(8,128)(2,1)} concatenate(bf16[2,1,2160]{1,2,0:T(8,128)(2,1)} %get-tuple-element.41, bf16[2,1,2160]{1,2,0:T(8,128)(2,1)} %get-tuple-element.40, bf16[2,1,2160]{1,2,0:T(8,128)(2,1)} %get-tuple-element.39, bf16[2,1,2160]{1,2,0:T(8,128)(2,1)} %get-tuple-element.38, bf16[2,1,2160]{1,2,0:T(8,128)(2,1)} %get-tuple-element.37, ...), dimensions={1} | concatenate | bytes 138240 | tf_op jit(solution)/shard_map/stack | solution.py:239
  105.4 9.2 %stack.102 = bf16[2,8,2160]{1,2,0:T(8,128)(2,1)} concatenate(bf16[2,1,2160]{1,2,0:T(8,128)(2,1)} %get-tuple-element.49, bf16[2,1,2160]{1,2,0:T(8,128)(2,1)} %get-tuple-element.48, bf16[2,1,2160]{1,2,0:T(8,128)(2,1)} %get-tuple-element.41, bf16[2,1,2160]{1,2,0:T(8,128)(2,1)} %get-tuple-element.40, bf16[2,1,2160]{1,2,0:T(8,128)(2,1)} %get-tuple-element.39, ...), dimensions={1} | concatenate | bytes 138240 | tf_op jit(solution)/shard_map/stack | solution.py:239
  114.5 8.4 %stack.110 = bf16[2,8,2160]{1,2,0:T(8,128)(2,1)} concatenate(bf16[2,1,2160]{1,2,0:T(8,128)(2,1)} %get-tuple-element.47, bf16[2,1,2160]{1,2,0:T(8,128)(2,1)} %get-tuple-element.46, bf16[2,1,2160]{1,2,0:T(8,128)(2,1)} %get-tuple-element.45, bf16[2,1,2160]{1,2,0:T(8,128)(2,1)} %get-tuple-element.44, bf16[2,1,2160]{1,2,0:T(8,128)(2,1)} %get-tuple-element.43, ...), dimensions={1} | concatenate | bytes 138240 | tf_op jit(solution)/shard_map/stack | solution.py:239
  123.0 7.9 %stack.100 = bf16[2,8,2160]{1,2,0:T(8,128)(2,1)S(1)} concatenate(bf16[2,1,2160]{1,2,0:T(8,128)(2,1)} %get-tuple-element.49, bf16[2,1,2160]{1,2,0:T(8,128)(2,1)} %get-tuple-element.48, bf16[2,1,2160]{1,2,0:T(8,128)(2,1)} %get-tuple-element.47, bf16[2,1,2160]{1,2,0:T(8,128)(2,1)} %get-tuple-element.46, bf16[2,1,2160]{1,2,0:T(8,128)(2,1)} %get-tuple-element.45, ...), dimensions={1} | concatenate | bytes 138240 | tf_op jit(solution)/shard_map/stack | solution.py:239
  130.9 1.1 bitcast_dynamic-update-slice_fusion.6
  132.0 0.5 copy-done.11
  132.6 1.1 bitcast_dynamic-update-slice_fusion.5
  133.6 0.6 copy-done.6
  134.3 0.3 copy-done.7
  134.6 8.4 %stack.104 = bf16[2,8,2160]{1,2,0:T(8,128)(2,1)} concatenate(bf16[2,1,2160]{1,2,0:T(8,128)(2,1)} %get-tuple-element.35, bf16[2,1,2160]{1,2,0:T(8,128)(2,1)} %get-tuple-element.34, bf16[2,1,2160]{1,2,0:T(8,128)(2,1)} %get-tuple-element.33, bf16[2,1,2160]{1,2,0:T(8,128)(2,1)} %get-tuple-element.32, bf16[2,1,2160]{1,2,0:T(8,128)(2,1)} %get-tuple-element.31, ...), dimensions={1} | concatenate | bytes 138240 | tf_op jit(solution)/shard_map/stack | solution.py:239
  143.0 2.5 %bitcast_dynamic-update-slice_fusion.4 = bf16[2,7,8,2160]{2,3,0,1:T(8,128)(2,1)} fusion(bf16[2,7,8,2160]{2,3,0,1:T(8,128)(2,1)} %bitcast_dynamic-update-slice_fusion.5, bf16[2,8,2160]{1,2,0:T(8,128)(2,1)} %stack.104), kind=kLoop, calls=%fused_computation.13 | loop fusion | bytes 2211840
  145.5 8.7 %stack.106 = bf16[2,8,2160]{1,2,0:T(8,128)(2,1)} concatenate(bf16[2,1,2160]{1,2,0:T(8,128)(2,1)} %get-tuple-element.27, bf16[2,1,2160]{1,2,0:T(8,128)(2,1)} %get-tuple-element.26, bf16[2,1,2160]{1,2,0:T(8,128)(2,1)} %get-tuple-element.25, bf16[2,1,2160]{1,2,0:T(8,128)(2,1)} %get-tuple-element.24, bf16[2,1,2160]{1,2,0:T(8,128)(2,1)} %get-tuple-element.23, ...), dimensions={1} | concatenate | bytes 138240 | tf_op jit(solution)/shard_map/stack | solution.py:239
  154.2 2.5 %bitcast_dynamic-update-slice_fusion.3 = bf16[2,7,8,2160]{2,3,0,1:T(8,128)(2,1)} fusion(bf16[2,7,8,2160]{2,3,0,1:T(8,128)(2,1)} %bitcast_dynamic-update-slice_fusion.4, bf16[2,8,2160]{1,2,0:T(8,128)(2,1)} %stack.106), kind=kLoop, calls=%fused_computation.12 | loop fusion | bytes 2211840
  156.8 8.4 %stack.108 = bf16[2,8,2160]{1,2,0:T(8,128)(2,1)} concatenate(bf16[2,1,2160]{1,2,0:T(8,128)(2,1)} %get-tuple-element.19, bf16[2,1,2160]{1,2,0:T(8,128)(2,1)} %get-tuple-element.18, bf16[2,1,2160]{1,2,0:T(8,128)(2,1)} %get-tuple-element.17, bf16[2,1,2160]{1,2,0:T(8,128)(2,1)} %get-tuple-element.16, bf16[2,1,2160]{1,2,0:T(8,128)(2,1)} %get-tuple-element.15, ...), dimensions={1} | concatenate | bytes 138240 | tf_op jit(solution)/shard_map/stack | solution.py:239
  165.2 2.4 %bitcast_dynamic-update-slice_fusion.2 = bf16[2,7,8,2160]{2,3,0,1:T(8,128)(2,1)} fusion(bf16[2,7,8,2160]{2,3,0,1:T(8,128)(2,1)} %bitcast_dynamic-update-slice_fusion.3, bf16[2,8,2160]{1,2,0:T(8,128)(2,1)} %stack.108), kind=kLoop, calls=%fused_computation.11 | loop fusion | bytes 2211840
  167.6 1.1 bitcast_dynamic-update-slice_fusion.1
  168.7 0.6 copy-done.9
  169.3 1.1 bitcast_dynamic-update-slice_fusion
  170.3 7.3 %copy.217 = bf16[2,7,8,2160]{3,0,1,2:T(2,128)(2,1)} copy(bf16[2,7,8,2160]{2,3,0,1:T(8,128)(2,1)} %bitcast_dynamic-update-slice_fusion) | data formatting | bytes 967680 | tf_op jit(solution)/shard_map/stack | solution.py:237
  177.6 8.6 %all-to-all-start = ((bf16[2,7,8,2160]{3,0,1,2:T(2,128)(2,1)}), bf16[2,7,8,2160]{3,0,1,2:T(2,128)(2,1)S(1)}, u32[]{:S(2)}, u32[]{:S(2)}) async-start(bf16[2,7,8,2160]{3,0,1,2:T(2,128)(2,1)} %copy.217), calls=%async_computation | async-start | bytes 974848 | tf_op jit(solution)/shard_map/all_to_all | solution.py:255
  186.2 0.1 reverse.4
  186.4 0.2 slice_reduce_fusion.4
  186.7 12.9 %all-to-all-done = bf16[2,7,8,2160]{3,0,1,2:T(2,128)(2,1)S(1)} async-done(((bf16[2,7,8,2160]{3,0,1,2:T(2,128)(2,1)}), bf16[2,7,8,2160]{3,0,1,2:T(2,128)(2,1)S(1)}, u32[]{:S(2)}, u32[]{:S(2)}) %all-to-all-start) | async-done | bytes 483872 | tf_op jit(solution)/shard_map/all_to_all | solution.py:255
  199.7 1.1 reshape_reshape.3
  200.8 0.7 fusion.44
  201.5 0.4 add_convert_fusion
  202.0 0.3 copy-done.12
  202.2 0.2 convolution_bitcast_fusion.1
  202.5 0.2 convolution_bitcast_fusion
  202.8 0.3 copy.228
  203.1 0.7 reshape.390
  203.8 0.2 fusion.45
  204.0 0.1 pad_maximum_fusion
  204.1 0.1 fusion.34
  204.2 0.1 concatenate.40
  204.4 0.2 concatenate.41
  204.6 0.8 copy.230
  (55 shorter events, 1.1 us)
Async XLA Ops:
  0.8 15.3 %collective-permute-start = (bf16[2,5712]{1,0:T(2,128)(2,1)S(1)}, bf16[2,5712]{1,0:T(2,128)(2,1)S(1)}, u32[]{:S(2)}, u32[]{:S(2)}) collective-permute-start(bf16[2,5712]{1,0:T(2,128)(2,1)S(1)} %slice.274), channel_id=1, source_target_pairs={{2,0},{4,2},{6,4},{8,6},{10,8},{12,10},{14,12},{3,1},{5,3},{7,5},{... | collective-permute-start | bytes 68552 | tf_op jit(solution)/shard_map/ppermute | solution.py:23
  4.5 0.7 copy-start.17
  4.5 0.9 copy-start.18
  105.4 9.2 %copy-start = (bf16[2,1,2160]{1,2,0:T(8,128)(2,1)S(1)}, bf16[2,1,2160]{1,2,0:T(8,128)(2,1)}, u32[]{:S(2)}) copy-start(bf16[2,1,2160]{1,2,0:T(8,128)(2,1)} %get-tuple-element.42) | copy-start | bytes 25924
  130.9 1.6 copy-start.11
  130.9 2.7 %copy-start.8 = (bf16[2,1,2160]{1,2,0:T(8,128)(2,1)S(1)}, bf16[2,1,2160]{1,2,0:T(8,128)(2,1)}, u32[]{:S(2)}) copy-start(bf16[2,1,2160]{1,2,0:T(8,128)(2,1)} %get-tuple-element.30) | copy-start | bytes 25924
  132.5 1.7 copy-start.6
  132.5 2.1 %copy-start.7 = (bf16[2,1,2160]{1,2,0:T(8,128)(2,1)S(1)}, bf16[2,1,2160]{1,2,0:T(8,128)(2,1)}, u32[]{:S(2)}) copy-start(bf16[2,1,2160]{1,2,0:T(8,128)(2,1)} %get-tuple-element.29) | copy-start | bytes 25924
  143.0 2.5 %copy-start.4 = (bf16[2,1,2160]{1,2,0:T(8,128)(2,1)S(1)}, bf16[2,1,2160]{1,2,0:T(8,128)(2,1)}, u32[]{:S(2)}) copy-start(bf16[2,1,2160]{1,2,0:T(8,128)(2,1)} %get-tuple-element.20) | copy-start | bytes 25924
  143.0 2.5 %copy-start.5 = (bf16[2,1,2160]{1,2,0:T(8,128)(2,1)S(1)}, bf16[2,1,2160]{1,2,0:T(8,128)(2,1)}, u32[]{:S(2)}) copy-start(bf16[2,1,2160]{1,2,0:T(8,128)(2,1)} %get-tuple-element.21) | copy-start | bytes 25924
  145.5 11.3 %copy-start.3 = (bf16[2,1,2160]{1,2,0:T(8,128)(2,1)S(1)}, bf16[2,1,2160]{1,2,0:T(8,128)(2,1)}, u32[]{:S(2)}) copy-start(bf16[2,1,2160]{1,2,0:T(8,128)(2,1)} %get-tuple-element.14) | copy-start | bytes 25924
  154.2 2.6 %copy-start.1 = (bf16[2,1,2160]{1,2,0:T(8,128)(2,1)S(1)}, bf16[2,1,2160]{1,2,0:T(8,128)(2,1)}, u32[]{:S(2)}) copy-start(bf16[2,1,2160]{1,2,0:T(8,128)(2,1)} %get-tuple-element.12) | copy-start | bytes 25924
  154.2 2.6 %copy-start.2 = (bf16[2,1,2160]{1,2,0:T(8,128)(2,1)S(1)}, bf16[2,1,2160]{1,2,0:T(8,128)(2,1)}, u32[]{:S(2)}) copy-start(bf16[2,1,2160]{1,2,0:T(8,128)(2,1)} %get-tuple-element.13) | copy-start | bytes 25924
  165.2 2.4 %copy-start.10 = (bf16[2,8,2160]{1,2,0:T(8,128)(2,1)S(1)}, bf16[2,8,2160]{1,2,0:T(8,128)(2,1)}, u32[]{:S(2)}) copy-start(bf16[2,8,2160]{1,2,0:T(8,128)(2,1)} %stack.110) | copy-start | bytes 207364
  167.6 1.6 copy-start.9
  177.6 8.8 %copy-start.16 = (f32[5,3456]{1,0:T(8,128)S(1)}, f32[5,3456]{1,0:T(8,128)}, u32[]{:S(2)}) copy-start(f32[5,3456]{1,0:T(8,128)} %param.7) | copy-start | bytes 207364
  177.6 22.0 %all-to-all-start = ((bf16[2,7,8,2160]{3,0,1,2:T(2,128)(2,1)}), bf16[2,7,8,2160]{3,0,1,2:T(2,128)(2,1)S(1)}, u32[]{:S(2)}, u32[]{:S(2)}) async-start(bf16[2,7,8,2160]{3,0,1,2:T(2,128)(2,1)} %copy.217), calls=%async_computation | async-start | bytes 974848 | tf_op jit(solution)/shard_map/all_to_all | solution.py:255
  201.5 0.7 copy-start.12
  201.5 0.7 copy-start.13
  201.5 0.9 copy-start.14
  201.5 0.9 copy-start.15

commit v2 on v1

v2 whole, which is shorter than its diff:
```python
import functools
import math

import jax
import jax.numpy as jnp
import numpy as np
from jax import lax
from jax.experimental import pallas as pl
from jax.experimental.pallas import tpu as pltpu
from jax.sharding import PartitionSpec as P

HOP = 432
FA = 27
FB = 128
KEEP = 2916
EDGE = 128
CH_DEV = 5


def shifted(value, axis, steps):
    count = lax.axis_size(axis)
    initial, last = (max(0, -steps), min(count, count - steps))
    return lax.ppermute(value, axis, [(source, source + steps) for source in range(initial, last)])


def angle_table(rows, cols, length):
    product = (
        jnp.arange(rows, dtype=jnp.int32)[:, None]
        * jnp.arange(cols, dtype=jnp.int32)[None, :]
        % length
    )
    return product.astype(jnp.float32) * (2.0 * math.pi / length)


def rotation_block(length):
    angles = angle_table(length, length, length)
    cosine_tab = jnp.cos(angles).astype(jnp.bfloat16)
    sine_tab = jnp.sin(angles).astype(jnp.bfloat16)
    return jnp.stack([jnp.stack([cosine_tab, sine_tab]), jnp.stack([-sine_tab, cosine_tab])])


def frame_view(segment, spectra, chan_len, hop_len):
    pieces = -(-chan_len // hop_len)
    framed = segment[:, : (spectra + pieces - 1) * hop_len].reshape(
        segment.shape[0], spectra + pieces - 1, hop_len
    )
    joined = jnp.concatenate(
        [framed[:, offset : offset + spectra] for offset in range(pieces)], axis=2
    )
    return joined[:, :, :chan_len]


def weighted_frames(signal, taps, spectra, hop_len):
    chan_len = taps.shape[1]
    running = jnp.zeros((2, spectra, chan_len), jnp.float32)
    for tap_index in range(taps.shape[0]):
        frames = frame_view(signal[:, tap_index * chan_len :], spectra, chan_len, hop_len)
        running = running + taps[tap_index][None, None, :] * frames.astype(jnp.float32)
    return running.astype(jnp.bfloat16)


def natural_order(series, section2_taps, radix_a, radix_b):
    tap_count, fine_len = section2_taps.shape
    items = series.shape[1]
    row_count = series.shape[2] // fine_len
    spectra = row_count - tap_count + 1
    row_blocks = series.reshape(2, items, row_count, fine_len)
    running = jnp.zeros((2, items, spectra, fine_len), jnp.float32)
    for tap_index in range(tap_count):
        running = running + section2_taps[tap_index] * row_blocks[
            :, :, tap_index : tap_index + spectra
        ].astype(jnp.float32)
    weighted = running.astype(jnp.bfloat16).reshape(2, items, spectra, radix_a, radix_b)
    return weighted, np.arange(radix_b)


def phase_order(received, section2_taps, radix_a, radix_b):
    tap_count, fine_len = section2_taps.shape
    sources, _, lines, rows = received.shape
    items = lines // GROUP
    short = fine_len // GROUP
    row_count = sources * rows // short
    spectra = row_count - tap_count + 1
    lanes = jnp.transpose(received, (1, 2, 0, 3)).reshape(2, items, GROUP, row_count, short)
    taps = jnp.transpose(section2_taps.reshape(tap_count, short, GROUP), (0, 2, 1))
    running = jnp.zeros((2, items, GROUP, spectra, short), jnp.float32)
    for tap_index in range(tap_count):
        running = running + taps[tap_index][:, None, :] * lanes[
            :, :, :, tap_index : tap_index + spectra
        ].astype(jnp.float32)
    inner = radix_b // GROUP
    weighted = running.astype(jnp.bfloat16).reshape(2, items, GROUP, spectra, radix_a, inner)
    weighted = jnp.transpose(weighted, (0, 1, 3, 4, 2, 5)).reshape(
        2, items, spectra, radix_a, radix_b
    )
    order = (np.arange(GROUP)[:, None] + GROUP * np.arange(inner)[None, :]).reshape(-1)
    return weighted, order


def ordered_angles(rows, order, length):
    product = (np.arange(rows)[:, None] * order[None, :] % length).astype(np.float32)
    return jnp.asarray(product) * (2.0 * math.pi / length)


def fine_spectra(weighted, order, keep_len, edge_len):
    _, items, spectra, radix_a, radix_b = weighted.shape
    fine_len = radix_a * radix_b
    partial_value = jnp.einsum(
        "pqkm,qcfmb->pcfkb", rotation_block(radix_a), weighted, preferred_element_type=jnp.float32
    )
    angles = ordered_angles(radix_a, order, fine_len)
    cosine_tab = jnp.cos(angles)
    sine_tab = jnp.sin(angles)
    real_part = partial_value[0] * cosine_tab + partial_value[1] * sine_tab
    imag_part = partial_value[1] * cosine_tab - partial_value[0] * sine_tab
    twiddled = jnp.concatenate([real_part, imag_part], axis=-1).astype(jnp.bfloat16)
    turned = ordered_angles(radix_b, order, radix_b).T
    cosine_b = jnp.cos(turned).astype(jnp.bfloat16)
    sine_b = jnp.sin(turned).astype(jnp.bfloat16)
    table = jnp.concatenate(
        [jnp.stack([cosine_b, -sine_b], axis=1), jnp.stack([sine_b, cosine_b], axis=1)], axis=0
    )
    spectrum = jnp.einsum(
        "cfkm,mpq->pcfqk", twiddled, table, preferred_element_type=jnp.float32
    ).reshape(2, items, spectra, fine_len)
    first = (-(keep_len // 2) - edge_len) % fine_len
    rest = keep_len + 2 * edge_len - (fine_len - first)
    return jnp.concatenate([spectrum[..., first:], spectrum[..., :rest]], axis=-1)


def stitch_bands(extended, upper_rim, lower_rim, slot_ids, band_width, keep_len, edge_len):
    centre = extended[..., edge_len : edge_len + keep_len]
    live = (slot_ids < band_width).astype(jnp.float32)[None, :, None, None]
    upper_ok = (slot_ids + 1 < band_width).astype(jnp.float32)[None, :, None, None]
    lower_ok = ((slot_ids >= 1) & (slot_ids < band_width)).astype(jnp.float32)[None, :, None, None]
    ramp = (jnp.arange(edge_len, dtype=jnp.float32) + 0.5) / (2.0 * edge_len)
    upper_weight = ramp * upper_ok
    lower_weight = ramp[::-1] * lower_ok
    low_part = centre[..., :edge_len] * (1.0 - lower_weight) + lower_rim * lower_weight
    high_part = centre[..., keep_len - edge_len :] * (1.0 - upper_weight) + upper_rim * upper_weight
    joined = jnp.concatenate(
        [low_part, centre[..., edge_len : keep_len - edge_len], high_part], axis=-1
    )
    return joined * live


GROUP = 8
CHUNK = 1152


def bank_kernel(turns, per_row, picks, x_ref, rim_ref, taps_ref, rot_ref, out_ref, data, bank, total, mix):
    step = pl.program_id(0)
    rows = x_ref.shape[1]
    halves = data.shape[0] // 2
    base = halves - rim_ref.shape[1]
    half = rot_ref.shape[1] // 2
    rot_len = rot_ref.shape[0]
    piece = 128

    @pl.when(step == 0)
    def _():
        total[...] = jnp.zeros_like(total)

    for part in range(2):
        data[pl.ds(part * halves, rows), :] = x_ref[part]
        data[pl.ds(part * halves + base, halves - base), :] = rim_ref[part]

    @pl.loop(0, CHUNK // piece)
    def _(index):
        row = pl.multiple_of(index * piece, piece)
        turn = pl.multiple_of((step * CHUNK + row) % rot_len, piece)
        wide = jnp.transpose(jnp.tile(taps_ref[:, pl.ds(row, piece)], (piece // GROUP, 1)))
        for col in range(0, 2 * half, piece):
            bank[pl.ds(row, piece), pl.ds(col, piece)] = (
                wide * rot_ref[pl.ds(turn, piece), pl.ds(col, piece)]
            ).astype(jnp.bfloat16)

    total[step // per_row] += jnp.dot(data[...], bank[...], preferred_element_type=jnp.float32)

    @pl.when(step == pl.num_programs(0) - 1)
    def _():
        for shift in range(1, turns):
            for part in range(2):
                total[shift, pl.ds(part * halves + rows, shift), :] = total[
                    shift, pl.ds(part * halves + base, shift), :
                ]
        for part in range(2):
            whole = jnp.zeros((rows, half), jnp.float32)
            for shift in range(turns):
                upper = total[shift, pl.ds(shift, rows), pl.ds(part * half, half)]
                lower = total[shift, pl.ds(halves + shift, rows), pl.ds((1 - part) * half, half)]
                whole += upper + lower if part == 0 else lower - upper
            mix[pl.ds(0, rows), :] = whole
            turned = jnp.transpose(mix[...])
            for dest, pick in enumerate(picks):
                out_ref[dest, part] = turned[
                    pick * GROUP : pick * GROUP + out_ref.shape[2], :rows
                ].astype(jnp.bfloat16)


def slot_bank(signal, following, taps, channels, spectra, picks, width):
    tap_count, chan_len = taps.shape
    row_len = GROUP * HOP
    rows = spectra // GROUP
    reach = (GROUP - 1) * HOP + tap_count * chan_len
    steps = -(-reach // CHUNK)
    per_row = row_len // CHUNK
    turns = -(-steps // per_row)
    rim = 16
    halves = -(-rows // 16) * 16 + rim
    data = signal.reshape(2, rows, row_len)
    fill = rim * row_len - following.shape[1]
    edge = jnp.pad(following, ((0, 0), (0, fill))).reshape(2, rim, row_len)
    flat = taps.reshape(-1)
    spread = jnp.stack(
        [
            jnp.pad(flat, (phase * HOP, steps * CHUNK - flat.shape[0] - phase * HOP))
            for phase in range(GROUP)
        ]
    )
    chans = channels.shape[0]
    half = GROUP * chans
    places = (np.arange(chan_len)[:, None] - HOP * np.arange(GROUP)[None, :]) % chan_len
    places = jnp.asarray(places.astype(np.int32))
    turns_of = (places[:, None, :] * channels[None, :, None]).reshape(chan_len, half) % chan_len
    angles = turns_of.astype(jnp.float32) * (2.0 * math.pi / chan_len)
    rot = jnp.concatenate([jnp.cos(angles), jnp.sin(angles)], axis=1)
    rot = rot.astype(jnp.bfloat16).astype(jnp.float32)
    deep = -(-rows // 128) * 128
    shape = (len(picks), 2, width * GROUP, rows)
    return pl.pallas_call(
        functools.partial(bank_kernel, turns, per_row, picks),
        grid=(steps,),
        in_specs=[
            pl.BlockSpec((2, rows, CHUNK), lambda i: (0, 0, i % per_row)),
            pl.BlockSpec((2, rim, CHUNK), lambda i: (0, 0, i % per_row)),
            pl.BlockSpec((GROUP, CHUNK), lambda i: (0, i)),
            pl.BlockSpec((chan_len, 2 * half), lambda i: (0, 0)),
        ],
        out_specs=pl.BlockSpec(shape, lambda i: (0, 0, 0, 0)),
        out_shape=jax.ShapeDtypeStruct(shape, jnp.bfloat16),
        scratch_shapes=[
            pltpu.VMEM((2 * halves, CHUNK), jnp.bfloat16),
            pltpu.VMEM((CHUNK, 2 * half), jnp.bfloat16),
            pltpu.VMEM((turns, 2 * halves, 2 * half), jnp.float32),
            pltpu.VMEM((deep, half), jnp.float32),
        ],
        name="slot_bank",
    )(data, edge, spread, rot)


def on_device(voltages, section1_taps, section2_taps, band_starts, band_widths):
    signal = voltages[0]
    tap_count, chan_len = section1_taps.shape
    spectra = signal.shape[1] // HOP
    rim_len = tap_count * chan_len - HOP
    tm_count = lax.axis_size("tm")
    zoom_count = lax.axis_size("zoom")
    device_count = tm_count * zoom_count
    slot_count = tm_count * CH_DEV
    width = CH_DEV + 2
    following = shifted(signal[:, :rim_len], ("tm", "zoom"), -1)
    span = slot_count + 2
    band_slots = jnp.arange(-1, slot_count + 1, dtype=jnp.int32)
    channels = ((band_starts[:, None] + band_slots[None, :]) % chan_len).reshape(-1)
    picks = [tm * CH_DEV + zoom * span for tm in range(tm_count) for zoom in range(zoom_count)]
    if channels.shape[0] <= 48 and spectra % GROUP == 0:
        filled = -(-channels.shape[0] // 16) * 16
        padded = jnp.pad(channels, (0, filled - channels.shape[0]))
        packed = slot_bank(signal, following, section1_taps, padded, spectra, picks, width)
        received = lax.all_to_all(packed, ("tm", "zoom"), split_axis=0, concat_axis=0, tiled=True)
        weighted, order = phase_order(received, section2_taps, FA, FB)
    else:
        pieces = -(-chan_len // HOP)
        padded = jnp.concatenate(
            [signal, following, jnp.zeros((2, pieces * HOP), jnp.bfloat16)], axis=1
        )
        frames = weighted_frames(padded, section1_taps, spectra, HOP)
        coarse = jnp.einsum(
            "pqkn,qsn->pks", rotation_block(chan_len), frames, preferred_element_type=jnp.float32
        ).astype(jnp.bfloat16)
        wanted = np.arange(width)[:, None] + np.asarray(picks)[None, :]
        packed = jnp.take(coarse, channels[wanted.reshape(-1)], axis=1)
        packed = packed.reshape(2, width, device_count, spectra)
        received = lax.all_to_all(packed, ("tm", "zoom"), split_axis=2, concat_axis=2, tiled=True)
        series = received.reshape(2, width, -1)
        weighted, order = natural_order(series, section2_taps, FA, FB)
    spans = fine_spectra(weighted, order, KEEP, EDGE)
    slot_ids = lax.axis_index("tm") * CH_DEV + jnp.arange(CH_DEV, dtype=jnp.int32)
    band_ids = jnp.arange(band_widths.shape[0], dtype=jnp.int32)
    band_width = jnp.sum(jnp.where(band_ids == lax.axis_index("zoom"), band_widths, 0))
    upper_rim = spans[:, 2:, :, :EDGE]
    lower_rim = spans[:, :CH_DEV, :, KEEP + EDGE :]
    extended = spans[:, 1 : CH_DEV + 1]
    stitched = stitch_bands(extended, upper_rim, lower_rim, slot_ids, band_width, KEEP, EDGE)
    fine_count = stitched.shape[2]
    result = jnp.transpose(stitched, (0, 2, 1, 3)).reshape(2, fine_count, CH_DEV * KEEP)
    return result[None, None]


def solution(mesh):
    placed = (P("pol", "groups", ("tm", "zoom")), P(), P(), P("groups"), P("groups"))
    return jax.shard_map(
        on_device,
        mesh=mesh,
        in_specs=placed,
        out_specs=P("pol", "zoom", "groups", None, "tm"),
        check_vma=False,
    )
```

time: 208 us -> 82.9 us (0.40); the launches traced: 205 us -> 82.5 us
  local copies, waits for them, and re-layouts: 122 us -> 23.1 us
  other arithmetic: 30.2 us -> 8.84 us
  Pallas kernels: 30 us -> 22.6 us
  waiting for transfers between devices: 12.9 us -> 17.5 us
    another operation x12 -> x4, local copies, waits for them, and re-layouts: 69.3 us -> 11.2 us  [the longest x1 10.2 us: slot_bank(): data = signal.reshape(2, rows, row_len)]
    slice x6 -> x0, local copies, waits for them, and re-layouts: 23.3 us -> none  [the longest x3 21.1 us: on_device(): coarse[:, int(index)]]
    concatenate x2 -> x0, other arithmetic: 20.6 us -> none  [the longest x1 20.6 us: on_device(): joined = jnp.concatenate([signal, following], axis=1)]
    unnamed x44 -> x13, local copies, waits for them, and re-layouts: 13.3 us -> 0.74 us
    pallas_call x1, Pallas kernels: 30 us -> 22.6 us  [slot_bank(): pl.pallas_call(functools.partial(bank_kernel, turns, per_row, picks), gri...]
    all_to_all x1, waiting for transfers between devices: 12.9 us -> 17.5 us  [on_device(): lax.all_to_all(packed, ('tm', 'zoom'), split_axis=0, concat_axis=0, tiled...]
    reshape x2 -> x3, local copies, waits for them, and re-layouts: 6.89 us -> 3.74 us  [the longest x1 2.28 us: phase_order(): jnp.transpose(received, (1, 2, 0, 3))]
    another operation x2 -> x1, local copies, waits for them, and re-layouts: 3.42 us -> 1.13 us  [slot_bank(): jnp.stack([jnp.pad(flat, (phase * HOP, steps * CHUNK - flat.shape[0] - ph...]
  transfers between devices with their start and end apart: 2 -> 2, of which waited for: 1 -> 1; matrix products, arithmetic and copies ran while one was open for 7% -> 27% of each run, Pallas kernels for 0% -> 0%
where the time goes in v2:
time: 82.9 us; the launch traced here: 82.5 us
  local copies, waits for them, and re-layouts  23.1 us (28%)
  Pallas kernels  22.6 us (27%)
  waiting for transfers between devices  17.5 us (21%)
  starting transfers between devices  9.72 us (12%)
  other arithmetic  8.84 us (11%)
    pallas_call x1, Pallas kernels, slot_bank(): pl.pallas_call(functools.partial(bank_kernel, turns, per_row, picks), gri...  22.6 us
    all_to_all x1, waiting for transfers between devices, on_device(): lax.all_to_all(packed, ('tm', 'zoom'), split_axis=0, concat_axis=0, tiled...  17.5 us
    another operation x1, local copies, waits for them, and re-layouts, slot_bank(): data = signal.reshape(2, rows, row_len)  10.2 us
    all_to_all x1, starting transfers between devices, on_device(): lax.all_to_all(packed, ('tm', 'zoom'), split_axis=0, concat_axis=0, tiled...  8.43 us
    another operation x2, other arithmetic  3.34 us
    reshape x1, local copies, waits for them, and re-layouts, phase_order(): jnp.transpose(received, (1, 2, 0, 3))  2.28 us
  transfers between devices with their start and end apart: 2, of which 1 were waited for; matrix products, arithmetic and copies ran while one was open for 27% of the time, Pallas kernels for 0%

profile of v2, /device:TPU:0, one launch (start us, length us, event | category | flops | bytes accessed | tf_op | source)
XLA Modules:
  0.0 82.5 jit_solution(5041950845450800704)
XLA Ops:
  0.0 0.8 slice.95
  0.8 1.3 %collective-permute-start = (bf16[2,5712]{1,0:T(2,128)(2,1)S(1)}, bf16[2,5712]{1,0:T(2,128)(2,1)S(1)}, u32[]{:S(2)}, u32[]{:S(2)}) collective-permute-start(bf16[2,5712]{1,0:T(2,128)(2,1)S(1)} %slice.95), channel_id=1, source_target_pairs={{2,0},{4,2},{6,4},{8,6},{10,8},{12,10},{14,12},{3,1},{5,3},{7,5},{... | collective-permute-start | bytes 68552 | tf_op jit(solution)/shard_map/ppermute | solution.py:23
  2.1 0.1 sine_convert_fusion.1
  2.2 0.1 fusion.24
  2.3 0.8 reshape.355
  3.1 0.1 fusion.30
  3.2 0.8 broadcast_bitcast_fusion
  4.0 0.3 copy.16
  4.3 0.0 copy-done.4
  4.3 0.1 broadcast_add_fusion
  4.3 0.1 add.148
  4.5 0.1 mul.305
  4.5 0.1 mul.306
  4.6 0.0 copy-done.1
  4.6 0.0 copy-start.5
  4.6 0.6 reshape.353
  5.3 0.1 slice_bitcast_fusion.4
  5.3 0.0 copy-done.5
  5.4 0.6 fusion.25
  6.0 0.6 compare_convert_fusion.1
  6.6 0.1 broadcast_reduce_fusion
  6.8 3.3 %cosine_convert_fusion = (bf16[512,384]{1,0:T(8,128)(2,1)S(1)}, bf16[512,384]{1,0:T(8,128)(2,1)S(1)}) fusion(s32[512,384]{1,0:T(8,128)S(1)} %copy.16, s32[384]{0:T(512)S(1)} %mul.306), kind=kLoop, calls=%fused_computation.10 | loop fusion | flops 3145728 | bytes 1574400 | tf_op jit(solution)/shard_map/convert.2
  10.1 1.3 %maximum_convert_fusion.rot_ref = f32[512,768]{1,0:T(8,128)} fusion(bf16[512,384]{1,0:T(8,128)(2,1)S(1)} %get-tuple-element.11, bf16[512,384]{1,0:T(8,128)(2,1)S(1)} %get-tuple-element.10), kind=kLoop, calls=%fused_computation.8 | loop fusion | flops 1572864 | bytes 2359296 | tf_op jit(solution)/shard_map/convert_element_type | solution.py:228
  11.3 0.6 compare_convert_fusion
  12.0 10.2 %reshape_squeeze.3.x_ref = bf16[2,270,3456]{2,1,0:T(8,128)(2,1)} reshape(bf16[1,2,933120]{2,1,0:T(2,128)(2,1)} %param.8) | data formatting | bytes 7464960 | tf_op jit(solution)/shard_map/reshape;squeeze | solution.py:211
  22.2 0.1 copy.15
  22.3 0.1 copy.18
  22.4 0.1 copy.19
  22.5 0.1 copy.20
  22.6 0.1 copy.21
  22.7 0.1 reverse.4
  22.8 0.1 mul.353
  22.9 1.1 %stack.75.taps_ref = f32[8,9216]{1,0:T(8,128)} concatenate(f32[1,9216]{1,0:T(1,128)S(1)} %bitcast.96, f32[1,9216]{1,0:T(1,128)S(1)} %bitcast.95, f32[1,9216]{1,0:T(1,128)S(1)} %bitcast.94, f32[1,9216]{1,0:T(1,128)S(1)} %bitcast.93, f32[1,9216]{1,0:T(1,128)S(1)} %bitcast.92, f32[1,9216]{1,0:T(1,128)S(1)} %bitcast.91, f32[1,9216]{1,0:T(1,128)S(1)} %bitcast.90, f32[1,9216]{1,0:T(1,128)S(1)} %bitcast.89), dimensions={0} | concatenate | bytes 589824 | tf_op jit(solution)/shard_map/stack | solution.py:215
  24.0 0.0 collective-permute-done
  24.0 0.1 pad.40
  24.2 0.7 copy.36
  24.9 22.6 %slot_bank.1 = bf16[8,2,56,270]{3,2,1,0:T(8,128)(2,1)} custom-call(bf16[2,270,3456]{2,1,0:T(8,128)(2,1)} %reshape_squeeze.3.x_ref, bf16[2,16,3456]{2,1,0:T(8,128)(2,1)} %bitcast.88, f32[8,9216]{1,0:T(8,128)} %stack.75.taps_ref, f32[512,768]{1,0:T(8,128)} %maximum_convert_fusion.rot_ref), custom_call_target="tpu_custom_call" | custom-call | tf_op jit(solution)/shard_map/slot_bank/pallas_call | solution.py:231
  47.4 8.4 %all-to-all-start = ((bf16[8,2,56,270]{3,2,1,0:T(8,128)(2,1)}), bf16[8,2,56,270]{3,2,1,0:T(8,128)(2,1)S(1)}, u32[]{:S(2)}, u32[]{:S(2)}) async-start(bf16[8,2,56,270]{3,2,1,0:T(8,128)(2,1)} %slot_bank.1), calls=%async_computation | async-start | bytes 1376256 | tf_op jit(solution)/shard_map/all_to_all | solution.py:271
  55.9 0.1 broadcast_subtract_fusion.1
  56.0 0.1 broadcast_subtract_fusion
  56.1 17.5 %all-to-all-done = bf16[8,2,56,270]{3,2,1,0:T(8,128)(2,1)S(1)} async-done(((bf16[8,2,56,270]{3,2,1,0:T(8,128)(2,1)}), bf16[8,2,56,270]{3,2,1,0:T(8,128)(2,1)S(1)}, u32[]{:S(2)}, u32[]{:S(2)}) %all-to-all-start) | async-done | bytes 483872 | tf_op jit(solution)/shard_map/all_to_all | solution.py:271
  73.6 0.1 copy.17
  73.7 2.3 %reshape.356 = bf16[2,7,8,5,432]{4,3,2,1,0:T(8,128)(2,1)S(1)} reshape(bf16[2,56,8,270]{3,2,1,0:T(8,128)(2,1)S(1)} %copy.17) | data formatting | bytes 967680 | tf_op jit(solution)/shard_map/reshape | solution.py:84
  76.0 1.6 %convert_reduce_fusion = bf16[2,7,8,432]{3,2,1,0:T(8,128)(2,1)S(1)} fusion(bf16[2,7,8,5,432]{4,3,2,1,0:T(8,128)(2,1)S(1)} %reshape.356, f32[8,432]{1,0:T(8,128)S(1)} %copy.21, f32[8,432]{1,0:T(8,128)S(1)} %copy.20, f32[8,432]{1,0:T(8,128)S(1)} %copy.19, f32[8,432]{1,0:T(8,128)S(1)} %copy.18, f32[8,432]{1,0:T(8,128)S(1)} %copy.15), kind=kLoop, calls=%fused_computation.26 | loop fusion | flops 725760 | bytes 649728 | tf_op jit(solution)/shard_map/convert_element_type | solution.py:92
  77.6 0.8 %reshape.357 = bf16[2,7,8,1,27,16]{5,4,2,1,0,3:T(8,128)(2,1)S(1)} reshape(bf16[2,7,8,432]{3,2,1,0:T(8,128)(2,1)S(1)} %convert_reduce_fusion) | data formatting | bytes 193536 | tf_op jit(solution)/shard_map/reshape | solution.py:92
  78.5 0.0 copy-start.2
  78.5 0.0 copy-start.3
  78.5 0.0 copy-start
  78.5 0.3 copy.31
  78.9 0.5 reshape.360
  79.4 0.2 convolution_bitcast_fusion.1
  79.6 0.0 copy-done.2
  79.6 0.0 copy-done.3
  79.7 0.0 copy-done
  79.7 0.2 convolution_bitcast_fusion
  79.9 0.3 copy.25
  80.2 0.7 reshape.359
  80.9 0.2 fusion.29
  81.1 0.1 pad_maximum_fusion
  81.2 0.1 fusion.22
  81.3 0.1 concatenate.28
  81.5 0.2 concatenate.29
  81.7 0.1 broadcast_multiply_fusion
  81.8 0.8 copy.27
  (11 shorter events, 0.1 us)
Async XLA Ops:
  0.0 4.3 %copy-start.4 = (s32[2]{0:T(128)S(1)}, s32[2]{0:T(128)}, u32[]{:S(2)}) copy-start(s32[2]{0:T(128)} %param.11) | copy-start | bytes 28
  0.0 4.6 %copy-start.1 = (f32[5,3456]{1,0:T(8,128)S(1)}, f32[5,3456]{1,0:T(8,128)}, u32[]{:S(2)}) copy-start(f32[5,3456]{1,0:T(8,128)} %param.10) | copy-start | bytes 207364
  0.8 23.3 %collective-permute-start = (bf16[2,5712]{1,0:T(2,128)(2,1)S(1)}, bf16[2,5712]{1,0:T(2,128)(2,1)S(1)}, u32[]{:S(2)}, u32[]{:S(2)}) collective-permute-start(bf16[2,5712]{1,0:T(2,128)(2,1)S(1)} %slice.95), channel_id=1, source_target_pairs={{2,0},{4,2},{6,4},{8,6},{10,8},{12,10},{14,12},{3,1},{5,3},{7,5},{... | collective-permute-start | bytes 68552 | tf_op jit(solution)/shard_map/ppermute | solution.py:23
  4.6 0.7 copy-start.5
  47.4 26.1 %all-to-all-start = ((bf16[8,2,56,270]{3,2,1,0:T(8,128)(2,1)}), bf16[8,2,56,270]{3,2,1,0:T(8,128)(2,1)S(1)}, u32[]{:S(2)}, u32[]{:S(2)}) async-start(bf16[8,2,56,270]{3,2,1,0:T(8,128)(2,1)} %slot_bank.1), calls=%async_computation | async-start | bytes 1376256 | tf_op jit(solution)/shard_map/all_to_all | solution.py:271
  78.5 1.2 %copy-start.2 = (f32[27,128]{1,0:T(8,128)S(1)}, f32[27,128]{1,0:T(8,128)}, u32[]{:S(2)}) copy-start(f32[27,128]{1,0:T(8,128)} %constant.114) | copy-start | bytes 41476
  78.5 1.2 %copy-start.3 = (f32[27,128]{1,0:T(8,128)S(1)}, f32[27,128]{1,0:T(8,128)}, u32[]{:S(2)}) copy-start(f32[27,128]{1,0:T(8,128)} %constant.115) | copy-start | bytes 41476
  78.5 1.2 %copy-start = (bf16[256,2,128,1]{2,0,3,1:T(8,128)(2,1)S(1)}, bf16[256,2,128,1]{2,0,3,1:T(8,128)(2,1)}, u32[]{:S(2)}) copy-start(bf16[256,2,128,1]{2,0,3,1:T(8,128)(2,1)} %constant.116) | copy-start | bytes 393220

commit v3 on v2

--- a/solution.py
+++ b/solution.py
@@ -15,6 +15,7 @@
 KEEP = 2916
 EDGE = 128
 CH_DEV = 5
+LIVE_DEV = 3
 
 
 def shifted(value, axis, steps):
@@ -148,7 +149,9 @@
 CHUNK = 1152
 
 
-def bank_kernel(turns, per_row, picks, x_ref, rim_ref, taps_ref, rot_ref, out_ref, data, bank, total, mix):
+def bank_kernel(
+    turns, per_row, pick_ref, x_ref, rim_ref, taps_ref, rot_ref, out_ref, tail_ref, data, bank, total, mix, turned
+):
     step = pl.program_id(0)
     rows = x_ref.shape[1]
     halves = data.shape[0] // 2
@@ -190,15 +193,27 @@
                 upper = total[shift, pl.ds(shift, rows), pl.ds(part * half, half)]
                 lower = total[shift, pl.ds(halves + shift, rows), pl.ds((1 - part) * half, half)]
                 whole += upper + lower if part == 0 else lower - upper
-            mix[pl.ds(0, rows), :] = whole
-            turned = jnp.transpose(mix[...])
-            for dest, pick in enumerate(picks):
-                out_ref[dest, part] = turned[
-                    pick * GROUP : pick * GROUP + out_ref.shape[2], :rows
-                ].astype(jnp.bfloat16)
-
-
-def slot_bank(signal, following, taps, channels, spectra, picks, width):
+            mix[pl.ds(0, rows), pl.ds(0, half)] = whole
+            turned[part] = jnp.transpose(mix[...])[:half]
+        dests, lines, main = out_ref.shape
+        width = lines // (2 * GROUP)
+        fill = -(-lines // 128) * 128 - lines
+
+        @pl.loop(0, dests)
+        def _(dest):
+            blocks = []
+            for part in range(2):
+                for slot in range(width):
+                    line = pl.multiple_of(pick_ref[dest * width + slot] * GROUP, GROUP)
+                    blocks.append(turned[part, pl.ds(line, GROUP), :])
+            block = jnp.concatenate(blocks, axis=0)
+            out_ref[dest] = block[:, :main].astype(jnp.bfloat16)
+            spare = jnp.zeros((fill, turned.shape[2] - main), jnp.float32)
+            rest = jnp.transpose(jnp.concatenate([block[:, main:], spare], axis=0))
+            tail_ref[dest] = rest[: tail_ref.shape[1], :lines].astype(jnp.bfloat16)
+
+
+def slot_bank(signal, following, taps, channels, spectra, picks):
     tap_count, chan_len = taps.shape
     row_len = GROUP * HOP
     rows = spectra // GROUP
@@ -227,26 +242,92 @@
     rot = jnp.concatenate([jnp.cos(angles), jnp.sin(angles)], axis=1)
     rot = rot.astype(jnp.bfloat16).astype(jnp.float32)
     deep = -(-rows // 128) * 128
-    shape = (len(picks), 2, width * GROUP, rows)
+    wide = -(-half // 128) * 128
+    main = rows // 128 * 128
+    lines = 2 * picks.shape[1] * GROUP
+    shape = (picks.shape[0], lines, main)
+    tail = (picks.shape[0], -(-(rows - main) // 16) * 16, lines)
     return pl.pallas_call(
-        functools.partial(bank_kernel, turns, per_row, picks),
-        grid=(steps,),
-        in_specs=[
-            pl.BlockSpec((2, rows, CHUNK), lambda i: (0, 0, i % per_row)),
-            pl.BlockSpec((2, rim, CHUNK), lambda i: (0, 0, i % per_row)),
-            pl.BlockSpec((GROUP, CHUNK), lambda i: (0, i)),
-            pl.BlockSpec((chan_len, 2 * half), lambda i: (0, 0)),
-        ],
-        out_specs=pl.BlockSpec(shape, lambda i: (0, 0, 0, 0)),
-        out_shape=jax.ShapeDtypeStruct(shape, jnp.bfloat16),
-        scratch_shapes=[
+        functools.partial(bank_kernel, turns, per_row),
+        out_shape=(
+            jax.ShapeDtypeStruct(shape, jnp.bfloat16),
+            jax.ShapeDtypeStruct(tail, jnp.bfloat16),
+        ),
+        grid_spec=pltpu.PrefetchScalarGridSpec(
+            num_scalar_prefetch=1,
+            grid=(steps,),
+            in_specs=[
+                pl.BlockSpec((2, rows, CHUNK), lambda i, p: (0, 0, i % per_row)),
+                pl.BlockSpec((2, rim, CHUNK), lambda i, p: (0, 0, i % per_row)),
+                pl.BlockSpec((GROUP, CHUNK), lambda i, p: (0, i)),
+                pl.BlockSpec((chan_len, 2 * half), lambda i, p: (0, 0)),
+            ],
+            out_specs=(
+                pl.BlockSpec(shape, lambda i, p: (0, 0, 0)),
+                pl.BlockSpec(tail, lambda i, p: (0, 0, 0)),
+            ),
+            scratch_shapes=[
             pltpu.VMEM((2 * halves, CHUNK), jnp.bfloat16),
             pltpu.VMEM((CHUNK, 2 * half), jnp.bfloat16),
             pltpu.VMEM((turns, 2 * halves, 2 * half), jnp.float32),
-            pltpu.VMEM((deep, half), jnp.float32),
+            pltpu.VMEM((deep, wide), jnp.float32),
+            pltpu.VMEM((2, half, deep), jnp.float32),
+            ],
+        ),
+        name="slot_bank",
+    )(picks.reshape(-1), data, edge, spread, rot)
+
+
+def swap_kernel(zooms, in_ref, in_tail, out_ref, out_tail, send_sems, recv_sems):
+    count = in_ref.shape[0]
+    me = lax.axis_index("tm") * zooms + lax.axis_index("zoom")
+    barrier = pltpu.get_barrier_semaphore()
+
+    def place(step):
+        other = lax.rem(me + step, count)
+        return other, {"tm": other // zooms, "zoom": lax.rem(other, zooms)}
+
+    for step in range(1, count):
+        pl.semaphore_signal(
+            barrier, inc=1, device_id=place(step)[1], device_id_type=pl.DeviceIdType.MESH
+        )
+    pl.semaphore_wait(barrier, count - 1)
+    copies = []
+    for step in range(1, count):
+        other, where = place(step)
+        for which, (source, target) in enumerate(((in_ref, out_ref), (in_tail, out_tail))):
+            copy = pltpu.make_async_remote_copy(
+                src_ref=source.at[other],
+                dst_ref=target.at[me],
+                send_sem=send_sems.at[which, step],
+                recv_sem=recv_sems.at[which, step],
+                device_id=where,
+                device_id_type=pl.DeviceIdType.MESH,
+            )
+            copy.start()
+            copies.append(copy)
+    out_ref[me] = in_ref[me]
+    out_tail[me] = in_tail[me]
+    for copy in copies:
+        copy.wait()
+
+
+def swapped(packed, tail, zooms, rows):
+    count, lines, main = packed.shape
+    body, rest = pl.pallas_call(
+        functools.partial(swap_kernel, zooms),
+        out_shape=tuple(jax.ShapeDtypeStruct(x.shape, x.dtype) for x in (packed, tail)),
+        in_specs=[pl.BlockSpec(memory_space=pltpu.VMEM)] * 2,
+        out_specs=(pl.BlockSpec(memory_space=pltpu.VMEM),) * 2,
+        scratch_shapes=[
+            pltpu.SemaphoreType.DMA((2, count)),
+            pltpu.SemaphoreType.DMA((2, count)),
         ],
-        name="slot_bank",
-    )(data, edge, spread, rot)
+        compiler_params=pltpu.CompilerParams(collective_id=0, has_side_effects=True),
+        name="swap_slots",
+    )(packed, tail)
+    rest = jnp.transpose(rest, (0, 2, 1))[:, :, : rows - main]
+    return jnp.concatenate([body, rest], axis=2).reshape(count, 2, lines // 2, rows)
 
 
 def on_device(voltages, section1_taps, section2_taps, band_starts, band_widths):
@@ -264,11 +345,21 @@
     band_slots = jnp.arange(-1, slot_count + 1, dtype=jnp.int32)
     channels = ((band_starts[:, None] + band_slots[None, :]) % chan_len).reshape(-1)
     picks = [tm * CH_DEV + zoom * span for tm in range(tm_count) for zoom in range(zoom_count)]
-    if channels.shape[0] <= 48 and spectra % GROUP == 0:
-        filled = -(-channels.shape[0] // 16) * 16
-        padded = jnp.pad(channels, (0, filled - channels.shape[0]))
-        packed = slot_bank(signal, following, section1_taps, padded, spectra, picks, width)
-        received = lax.all_to_all(packed, ("tm", "zoom"), split_axis=0, concat_axis=0, tiled=True)
+    live_count = LIVE_DEV * device_count
+    ragged = spectra // GROUP % 128
+    if live_count <= 48 and spectra % GROUP == 0 and spectra // GROUP > 128 and ragged:
+        band_ends = jnp.cumsum(band_widths)
+        band_firsts = band_ends - band_widths
+        live_ids = jnp.arange(live_count, dtype=jnp.int32)
+        band_of = jnp.sum((band_ends[None, :] <= live_ids[:, None]).astype(jnp.int32), axis=1)
+        member = band_of[:, None] == jnp.arange(zoom_count, dtype=jnp.int32)[None, :]
+        shifts = jnp.where(member, (band_starts - band_firsts)[None, :], 0)
+        channels = (jnp.sum(shifts, axis=1) + live_ids) % chan_len
+        slots = np.arange(tm_count)[:, None, None] * CH_DEV + np.arange(-1, CH_DEV + 1)
+        slots = jnp.asarray(slots.astype(np.int32)) + band_firsts[None, :, None]
+        lines = jnp.clip(slots, 0, live_count - 1).reshape(device_count, width)
+        packed, tail = slot_bank(signal, following, section1_taps, channels, spectra, lines)
+        received = swapped(packed, tail, zoom_count, spectra // GROUP)
         weighted, order = phase_order(received, section2_taps, FA, FB)
     else:
         pieces = -(-chan_len // HOP)

time: 82.9 us -> 75.4 us (0.910)
  waiting for transfers between devices: 17.5 us -> 0.01 us
  Pallas kernels: 22.6 us -> 37.5 us
  starting transfers between devices: 9.72 us -> 1.29 us
  other arithmetic: 8.84 us -> 10.3 us
  local copies, waits for them, and re-layouts: 23.1 us -> 24.5 us
    all_to_all x1 -> x0, waiting for transfers between devices: 17.5 us -> none  [on_device(): lax.all_to_all(packed, ('tm', 'zoom'), split_axis=0, concat_axis=0, tiled...]
    pallas_call x1 -> x2, Pallas kernels: 22.6 us -> 37.5 us  [the longest x1 20.1 us: slot_bank(): pl.pallas_call(functools.partial(bank_kernel, turns, per_row), out_shape=...]
    all_to_all x1 -> x0, starting transfers between devices: 8.43 us -> none  [on_device(): lax.all_to_all(packed, ('tm', 'zoom'), split_axis=0, concat_axis=0, tiled...]
    sub x0 -> x1, other arithmetic: none -> 1.31 us  [on_device(): shifts = jnp.where(member, (band_starts - band_firsts)[None, :], 0)]
    concatenate x0 -> x1, other arithmetic: none -> 1.09 us  [swapped(): jnp.concatenate([body, rest], axis=2).reshape(count, 2, lines // 2, rows)]
    slice x0 -> x1, local copies, waits for them, and re-layouts: none -> 0.94 us  [swapped(): rest = jnp.transpose(rest, (0, 2, 1))[:, :, :rows - main]]
    another operation x2 -> x3, other arithmetic: 3.34 us -> 3.07 us
  transfers between devices with their start and end apart: 2 -> 1, of which waited for: 1 -> 0; matrix products, arithmetic and copies ran while one was open for 27% -> 31% of each run, Pallas kernels for 0% -> 0%
where the time goes in v3:
time: 75.4 us; the launch traced here: 74.3 us
  Pallas kernels  37.5 us (50%)
  local copies, waits for them, and re-layouts  24.5 us (32%)
  other arithmetic  10.3 us (14%)
  starting transfers between devices  1.29 us (2%)
    pallas_call x1, Pallas kernels, slot_bank(): pl.pallas_call(functools.partial(bank_kernel, turns, per_row), out_shape=...  20.1 us
    pallas_call x1, Pallas kernels, swapped(): pl.pallas_call(functools.partial(swap_kernel, zooms), out_shape=tuple((ja...  17.4 us
    another operation x1, local copies, waits for them, and re-layouts, slot_bank(): data = signal.reshape(2, rows, row_len)  10.2 us
    another operation x3, other arithmetic  3.07 us
    reshape x1, local copies, waits for them, and re-layouts, phase_order(): jnp.transpose(received, (1, 2, 0, 3))  2.28 us
    convert_element_type x1, other arithmetic, phase_order(): running.astype(jnp.bfloat16)  1.59 us
  transfers between devices with their start and end apart: 1, of which 0 were waited for; matrix products, arithmetic and copies ran while one was open for 31% of the time, Pallas kernels for 0%

profile of v3, /device:TPU:0, one launch (start us, length us, event | category | flops | bytes accessed | tf_op | source)
XLA Modules:
  0.0 74.3 jit_solution(9446874527234557201)
XLA Ops:
  0.0 0.8 %slice.99 = bf16[2,5712]{1,0:T(2,128)(2,1)S(1)} slice(bf16[2,933120]{1,0:T(2,128)(2,1)} %bitcast.93), slice={[0:2], [0:5712]} | slice | bytes 45696 | tf_op jit(solution)/shard_map/slice | solution.py:343
  0.8 1.3 %collective-permute-start = (bf16[2,5712]{1,0:T(2,128)(2,1)S(1)}, bf16[2,5712]{1,0:T(2,128)(2,1)S(1)}, u32[]{:S(2)}, u32[]{:S(2)}) collective-permute-start(bf16[2,5712]{1,0:T(2,128)(2,1)S(1)} %slice.99), channel_id=1, source_target_pairs={{2,0},{4,2},{6,4},{8,6},{10,8},{12,10},{14,12},{3,1},{5,3},{7,5},{... | collective-permute-start | bytes 68552 | tf_op jit(solution)/shard_map/ppermute | solution.py:24
  2.1 0.1 sine_convert_fusion.1
  2.2 0.1 fusion.24
  2.3 0.8 %reduce-window.8 = s32[2,1]{0,1:T(1,128)S(1)} reduce-window(s32[2,1]{0,1:T(1,128)} %bitcast.108, s32[]{:T(128)} %constant.62.clone.1), window={size=2x1 pad=1_0x0_0}, to_apply=%region_0.0 | reduce-window | flops 2 | bytes 20 | tf_op jit(solution)/shard_map/reduce-window.3
  3.1 1.3 %fusion.31 = (s32[2]{0:T(128)S(1)}, s32[2]{0:T(128)S(1)}, s32[]{:T(128)}) fusion(s32[2]{0:T(128)} %param.12, s32[2]{0:T(128)} %param.13, s32[2,1]{0,1:T(1,128)S(1)} %reduce-window.8, s32[]{:T(128)S(6)} %axis_index.28), kind=kLoop, calls=%fused_computation.91 | loop fusion | flops 9 | bytes 48 | tf_op jit(solution)/shard_map/sub | solution.py:356
  4.4 0.6 compare_convert_fusion
  5.1 0.7 compare_convert_fusion.2
  5.8 0.8 %reshape.399 = f32[6144]{0:T(1024)S(1)} reshape(f32[12,512]{1,0:T(8,128)} %param.10) | data formatting | bytes 49152 | tf_op jit(solution)/shard_map/reshape | solution.py:229
  6.5 0.1 fusion.33
  6.6 0.1 fusion.25
  6.7 0.1 fusion.26
  6.8 0.1 mul.305
  6.9 0.1 mul.306
  7.0 0.8 %broadcast_bitcast_fusion = s32[512,192]{0,1:T(8,128)S(1)} fusion(s32[512,8]{0,1:T(8,128)} %constant.81.clone), kind=kLoop, calls=%fused_computation.34 | loop fusion | bytes 409600 | tf_op jit(solution)/shard_map/mul | solution.py:240
  7.8 0.2 copy.32
  8.0 0.0 copy-done.1
  8.0 0.6 reshape.395
  8.6 0.1 slice_bitcast_fusion.4
  8.7 0.0 copy-start.4
  8.7 0.1 reverse.4
  8.8 0.1 broadcast_reduce_fusion
  8.9 2.2 %cosine_convert_fusion = (bf16[512,192]{1,0:T(8,128)(2,1)S(1)}, bf16[512,192]{1,0:T(8,128)(2,1)S(1)}) fusion(s32[512,192]{1,0:T(8,128)S(1)} %copy.32, s32[192]{0:T(256)S(1)} %mul.306), kind=kLoop, calls=%fused_computation.11 | loop fusion | flops 1572864 | bytes 787200 | tf_op jit(solution)/shard_map/convert.2
  11.1 1.0 %maximum_convert_fusion.rot_ref = f32[512,384]{1,0:T(8,128)} fusion(bf16[512,192]{1,0:T(8,128)(2,1)S(1)} %get-tuple-element.21, bf16[512,192]{1,0:T(8,128)(2,1)S(1)} %get-tuple-element.20), kind=kLoop, calls=%fused_computation.12 | loop fusion | flops 786432 | bytes 1179648 | tf_op jit(solution)/shard_map/convert_element_type | solution.py:243
  12.2 0.0 copy-done.4
  12.2 0.1 add_clamp_fusion
  12.2 0.1 broadcast_subtract_fusion.1
  12.3 0.1 broadcast_subtract_fusion
  12.4 10.2 %reshape_squeeze.3.x_ref = bf16[2,270,3456]{2,1,0:T(8,128)(2,1)} reshape(bf16[1,2,933120]{2,1,0:T(2,128)(2,1)} %param.9) | data formatting | bytes 7464960 | tf_op jit(solution)/shard_map/reshape;squeeze | solution.py:226
  22.6 0.6 min.12.pick_ref
  23.2 0.1 copy.31
  23.3 0.1 copy.35
  23.4 0.1 copy.36
  23.5 0.1 copy.37
  23.6 0.1 copy.38
  23.7 0.1 mul.353
  23.8 1.1 %stack.75.taps_ref = f32[8,9216]{1,0:T(8,128)} concatenate(f32[1,9216]{1,0:T(1,128)S(1)} %bitcast.106, f32[1,9216]{1,0:T(1,128)S(1)} %bitcast.105, f32[1,9216]{1,0:T(1,128)S(1)} %bitcast.104, f32[1,9216]{1,0:T(1,128)S(1)} %bitcast.103, f32[1,9216]{1,0:T(1,128)S(1)} %bitcast.102, f32[1,9216]{1,0:T(1,128)S(1)} %bitcast.101, f32[1,9216]{1,0:T(1,128)S(1)} %bitcast.100, ...), dimensions={0} | concatenate | bytes 589824 | tf_op jit(solution)/shard_map/stack | solution.py:230
  24.9 0.0 collective-permute-done
  24.9 0.1 pad.36
  25.1 0.7 copy.55
  25.8 20.1 %slot_bank.1 = (bf16[8,112,256]{2,1,0:T(8,128)(2,1)}, bf16[8,16,112]{2,1,0:T(8,128)(2,1)}) custom-call(s32[56]{0:T(128)} %min.12.pick_ref, bf16[2,270,3456]{2,1,0:T(8,128)(2,1)} %reshape_squeeze.3.x_ref, bf16[2,16,3456]{2,1,0:T(8,128)(2,1)} %bitcast.98, f32[8,9216]{1,0:T(8,128)} %stack.75.taps_ref, f32[512,384]{1,0:T(8,128)} %maximum_convert_fusion.rot_ref), custom_call_target="tpu_custom_call" | custom-call | tf_op jit(solution)/shard_map/slot_bank/pallas_call | solution.py:250
  45.8 17.4 %swap_slots.1 = (bf16[8,112,256]{2,1,0:T(8,128)(2,1)}, bf16[8,16,112]{2,1,0:T(8,128)(2,1)}) custom-call(bf16[8,112,256]{2,1,0:T(8,128)(2,1)} %get-tuple-element.9.in_ref, bf16[8,16,112]{2,1,0:T(8,128)(2,1)} %get-tuple-element.10.in_tail), custom_call_target="tpu_custom_call" | custom-call | tf_op jit(solution)/shard_map/swap_slots/pallas_call | solution.py:317
  63.3 0.9 %copy.33 = bf16[8,112,14]{2,1,0:T(8,128)(2,1)S(1)} copy(bf16[8,112,14]{1,2,0:T(8,128)(2,1)} %bitcast.107) | data formatting | bytes 50176 | tf_op jit(solution)/shard_map/slice | solution.py:329
  64.2 1.1 %pad_maximum_fusion = bf16[8,112,270]{2,1,0:T(8,128)(2,1)S(1)} fusion(bf16[8,112,14]{2,1,0:T(8,128)(2,1)S(1)} %copy.33, bf16[8,112,256]{2,1,0:T(8,128)(2,1)} %get-tuple-element.11), kind=kLoop, calls=%fused_computation.5 | loop fusion | flops 967680 | bytes 967680 | tf_op jit(solution)/shard_map/concatenate | solution.py:330
  65.3 0.1 copy.54
  65.5 2.3 %reshape.401 = bf16[2,7,8,5,432]{4,3,2,1,0:T(8,128)(2,1)S(1)} reshape(bf16[2,56,8,270]{3,2,1,0:T(8,128)(2,1)S(1)} %bitcast.96) | data formatting | bytes 967680 | tf_op jit(solution)/shard_map/reshape | solution.py:85
  67.8 1.6 %convert_reduce_fusion = bf16[2,7,8,432]{3,2,1,0:T(8,128)(2,1)S(1)} fusion(bf16[2,7,8,5,432]{4,3,2,1,0:T(8,128)(2,1)S(1)} %reshape.401, f32[8,432]{1,0:T(8,128)S(1)} %copy.38, f32[8,432]{1,0:T(8,128)S(1)} %copy.37, f32[8,432]{1,0:T(8,128)S(1)} %copy.36, f32[8,432]{1,0:T(8,128)S(1)} %copy.35, f32[8,432]{1,0:T(8,128)S(1)} %copy.31), kind=kLoop, calls=%fused_computation.27 | loop fusion | flops 725760 | bytes 649728 | tf_op jit(solution)/shard_map/convert_element_type | solution.py:93
  69.3 0.8 %reshape.402 = bf16[2,7,8,1,27,16]{5,4,2,1,0,3:T(8,128)(2,1)S(1)} reshape(bf16[2,7,8,432]{3,2,1,0:T(8,128)(2,1)S(1)} %convert_reduce_fusion) | data formatting | bytes 193536 | tf_op jit(solution)/shard_map/reshape | solution.py:93
  70.2 0.0 copy-start.2
  70.2 0.0 copy-start.3
  70.2 0.0 copy-start
  70.2 0.3 copy.48
  70.6 0.5 reshape.405
  71.1 0.2 convolution_bitcast_fusion.1
  71.4 0.2 convolution_bitcast_fusion
  71.6 0.3 copy.42
  72.0 0.7 reshape.404
  72.7 0.2 fusion.32
  72.8 0.1 pad_maximum_fusion.1
  73.0 0.1 fusion.22
  73.1 0.1 concatenate.32
  73.2 0.2 concatenate.33
  73.4 0.1 broadcast_multiply_fusion
  73.5 0.8 %copy.44 = f32[1,1,2,1,14580]{4,3,2,1,0:T(1,128)} copy(f32[1,1,2,1,14580]{4,2,3,1,0:T(2,128)S(1)} %broadcast_multiply_fusion) | data formatting | bytes 233280 | tf_op jit(solution)/shard_map/mul | solution.py:145
  (11 shorter events, 0.1 us)
Async XLA Ops:
  0.0 8.0 %copy-start.1 = (f32[5,3456]{1,0:T(8,128)S(1)}, f32[5,3456]{1,0:T(8,128)}, u32[]{:S(2)}) copy-start(f32[5,3456]{1,0:T(8,128)} %param.11) | copy-start | bytes 207364
  0.8 24.2 %collective-permute-start = (bf16[2,5712]{1,0:T(2,128)(2,1)S(1)}, bf16[2,5712]{1,0:T(2,128)(2,1)S(1)}, u32[]{:S(2)}, u32[]{:S(2)}) collective-permute-start(bf16[2,5712]{1,0:T(2,128)(2,1)S(1)} %slice.99), channel_id=1, source_target_pairs={{2,0},{4,2},{6,4},{8,6},{10,8},{12,10},{14,12},{3,1},{5,3},{7,5},{... | collective-permute-start | bytes 68552 | tf_op jit(solution)/shard_map/ppermute | solution.py:24
  8.7 3.5 %copy-start.4 = (s32[4,7]{1,0:T(4,128)S(1)}, s32[4,7]{1,0:T(4,128)}, u32[]{:S(2)}) copy-start(s32[4,7]{1,0:T(4,128)} %constant.117) | copy-start | bytes 340
  70.2 1.2 %copy-start.2 = (f32[27,128]{1,0:T(8,128)S(1)}, f32[27,128]{1,0:T(8,128)}, u32[]{:S(2)}) copy-start(f32[27,128]{1,0:T(8,128)} %constant.119) | copy-start | bytes 41476
  70.2 1.2 %copy-start.3 = (f32[27,128]{1,0:T(8,128)S(1)}, f32[27,128]{1,0:T(8,128)}, u32[]{:S(2)}) copy-start(f32[27,128]{1,0:T(8,128)} %constant.120) | copy-start | bytes 41476
  70.2 1.2 %copy-start = (bf16[256,2,128,1]{2,0,3,1:T(8,128)(2,1)S(1)}, bf16[256,2,128,1]{2,0,3,1:T(8,128)(2,1)}, u32[]{:S(2)}) copy-start(bf16[256,2,128,1]{2,0,3,1:T(8,128)(2,1)} %constant.121) | copy-start | bytes 393220

commit v4 on v3

--- a/solution.py
+++ b/solution.py
@@ -154,7 +154,7 @@
 ):
     step = pl.program_id(0)
     rows = x_ref.shape[1]
-    halves = data.shape[0] // 2
+    halves = data.shape[1] // 2
     base = halves - rim_ref.shape[1]
     half = rot_ref.shape[1] // 2
     rot_len = rot_ref.shape[0]
@@ -164,9 +164,11 @@
     def _():
         total[...] = jnp.zeros_like(total)
 
-    for part in range(2):
-        data[pl.ds(part * halves, rows), :] = x_ref[part]
-        data[pl.ds(part * halves + base, halves - base), :] = rim_ref[part]
+    @pl.when(step < per_row)
+    def _():
+        for part in range(2):
+            data[step, pl.ds(part * halves, rows), :] = x_ref[part]
+            data[step, pl.ds(part * halves + base, halves - base), :] = rim_ref[part]
 
     @pl.loop(0, CHUNK // piece)
     def _(index):
@@ -178,7 +180,9 @@
                 wide * rot_ref[pl.ds(turn, piece), pl.ds(col, piece)]
             ).astype(jnp.bfloat16)
 
-    total[step // per_row] += jnp.dot(data[...], bank[...], preferred_element_type=jnp.float32)
+    total[step // per_row] += jnp.dot(
+        data[step % per_row], bank[...], preferred_element_type=jnp.float32
+    )
 
     @pl.when(step == pl.num_programs(0) - 1)
     def _():
@@ -257,8 +261,8 @@
             num_scalar_prefetch=1,
             grid=(steps,),
             in_specs=[
-                pl.BlockSpec((2, rows, CHUNK), lambda i, p: (0, 0, i % per_row)),
-                pl.BlockSpec((2, rim, CHUNK), lambda i, p: (0, 0, i % per_row)),
+                pl.BlockSpec((2, rows, CHUNK), lambda i, p: (0, 0, jnp.minimum(i, per_row - 1))),
+                pl.BlockSpec((2, rim, CHUNK), lambda i, p: (0, 0, jnp.minimum(i, per_row - 1))),
                 pl.BlockSpec((GROUP, CHUNK), lambda i, p: (0, i)),
                 pl.BlockSpec((chan_len, 2 * half), lambda i, p: (0, 0)),
             ],
@@ -267,7 +271,7 @@
                 pl.BlockSpec(tail, lambda i, p: (0, 0, 0)),
             ),
             scratch_shapes=[
-            pltpu.VMEM((2 * halves, CHUNK), jnp.bfloat16),
+            pltpu.VMEM((per_row, 2 * halves, CHUNK), jnp.bfloat16),
             pltpu.VMEM((CHUNK, 2 * half), jnp.bfloat16),
             pltpu.VMEM((turns, 2 * halves, 2 * half), jnp.float32),
             pltpu.VMEM((deep, wide), jnp.float32),

time: 75.4 us -> 75 us (level)
  no operation moved by 1% of the time
where the time goes in v4:
time: 75 us; the launch traced here: 73.8 us
  Pallas kernels  37 us (49%)
  local copies, waits for them, and re-layouts  24.5 us (33%)
  other arithmetic  10.3 us (14%)
  starting transfers between devices  1.29 us (2%)
    pallas_call x1, Pallas kernels, slot_bank(): pl.pallas_call(functools.partial(bank_kernel, turns, per_row), out_shape=...  19.6 us
    pallas_call x1, Pallas kernels, swapped(): pl.pallas_call(functools.partial(swap_kernel, zooms), out_shape=tuple((ja...  17.4 us
    another operation x1, local copies, waits for them, and re-layouts, slot_bank(): data = signal.reshape(2, rows, row_len)  10.2 us
    another operation x3, other arithmetic  3.07 us
    reshape x1, local copies, waits for them, and re-layouts, phase_order(): jnp.transpose(received, (1, 2, 0, 3))  2.28 us
    convert_element_type x1, other arithmetic, phase_order(): running.astype(jnp.bfloat16)  1.59 us
  transfers between devices with their start and end apart: 1, of which 0 were waited for; matrix products, arithmetic and copies ran while one was open for 31% of the time, Pallas kernels for 0%

profile of v4, /device:TPU:0, one launch (start us, length us, event | category | flops | bytes accessed | tf_op | source)
XLA Modules:
  0.0 73.8 jit_solution(1923377943812660629)
XLA Ops:
  0.0 0.8 %slice.99 = bf16[2,5712]{1,0:T(2,128)(2,1)S(1)} slice(bf16[2,933120]{1,0:T(2,128)(2,1)} %bitcast.93), slice={[0:2], [0:5712]} | slice | bytes 45696 | tf_op jit(solution)/shard_map/slice | solution.py:347
  0.8 1.3 %collective-permute-start = (bf16[2,5712]{1,0:T(2,128)(2,1)S(1)}, bf16[2,5712]{1,0:T(2,128)(2,1)S(1)}, u32[]{:S(2)}, u32[]{:S(2)}) collective-permute-start(bf16[2,5712]{1,0:T(2,128)(2,1)S(1)} %slice.99), channel_id=1, source_target_pairs={{2,0},{4,2},{6,4},{8,6},{10,8},{12,10},{14,12},{3,1},{5,3},{7,5},{... | collective-permute-start | bytes 68552 | tf_op jit(solution)/shard_map/ppermute | solution.py:24
  2.1 0.1 sine_convert_fusion.1
  2.2 0.1 fusion.24
  2.3 0.8 %reduce-window.8 = s32[2,1]{0,1:T(1,128)S(1)} reduce-window(s32[2,1]{0,1:T(1,128)} %bitcast.108, s32[]{:T(128)} %constant.62.clone.1), window={size=2x1 pad=1_0x0_0}, to_apply=%region_0.0 | reduce-window | flops 2 | bytes 20 | tf_op jit(solution)/shard_map/reduce-window.3
  3.1 1.3 %fusion.31 = (s32[2]{0:T(128)S(1)}, s32[2]{0:T(128)S(1)}, s32[]{:T(128)}) fusion(s32[2]{0:T(128)} %param.12, s32[2]{0:T(128)} %param.13, s32[2,1]{0,1:T(1,128)S(1)} %reduce-window.8, s32[]{:T(128)S(6)} %axis_index.28), kind=kLoop, calls=%fused_computation.91 | loop fusion | flops 9 | bytes 48 | tf_op jit(solution)/shard_map/sub | solution.py:360
  4.4 0.6 compare_convert_fusion
  5.1 0.7 compare_convert_fusion.2
  5.8 0.8 %reshape.399 = f32[6144]{0:T(1024)S(1)} reshape(f32[12,512]{1,0:T(8,128)} %param.10) | data formatting | bytes 49152 | tf_op jit(solution)/shard_map/reshape | solution.py:233
  6.5 0.1 fusion.33
  6.6 0.1 fusion.25
  6.7 0.1 fusion.26
  6.8 0.1 mul.305
  6.9 0.1 mul.306
  7.0 0.8 %broadcast_bitcast_fusion = s32[512,192]{0,1:T(8,128)S(1)} fusion(s32[512,8]{0,1:T(8,128)} %constant.81.clone), kind=kLoop, calls=%fused_computation.34 | loop fusion | bytes 409600 | tf_op jit(solution)/shard_map/mul | solution.py:244
  7.8 0.2 copy.32
  8.0 0.6 reshape.395
  8.6 0.1 slice_bitcast_fusion.4
  8.7 0.0 copy-start.4
  8.7 0.1 reverse.4
  8.8 0.1 broadcast_reduce_fusion
  8.9 2.2 %cosine_convert_fusion = (bf16[512,192]{1,0:T(8,128)(2,1)S(1)}, bf16[512,192]{1,0:T(8,128)(2,1)S(1)}) fusion(s32[512,192]{1,0:T(8,128)S(1)} %copy.32, s32[192]{0:T(256)S(1)} %mul.306), kind=kLoop, calls=%fused_computation.11 | loop fusion | flops 1572864 | bytes 787200 | tf_op jit(solution)/shard_map/convert.2
  11.1 1.0 %maximum_convert_fusion.rot_ref = f32[512,384]{1,0:T(8,128)} fusion(bf16[512,192]{1,0:T(8,128)(2,1)S(1)} %get-tuple-element.21, bf16[512,192]{1,0:T(8,128)(2,1)S(1)} %get-tuple-element.20), kind=kLoop, calls=%fused_computation.12 | loop fusion | flops 786432 | bytes 1179648 | tf_op jit(solution)/shard_map/convert_element_type | solution.py:247
  12.2 0.1 add_clamp_fusion
  12.2 0.1 broadcast_subtract_fusion.1
  12.3 0.1 broadcast_subtract_fusion
  12.4 10.2 %reshape_squeeze.3.x_ref = bf16[2,270,3456]{2,1,0:T(8,128)(2,1)} reshape(bf16[1,2,933120]{2,1,0:T(2,128)(2,1)} %param.9) | data formatting | bytes 7464960 | tf_op jit(solution)/shard_map/reshape;squeeze | solution.py:230
  22.6 0.6 min.12.pick_ref
  23.2 0.1 copy.31
  23.3 0.1 copy.35
  23.4 0.1 copy.36
  23.5 0.1 copy.37
  23.6 0.1 copy.38
  23.7 0.1 mul.353
  23.8 1.1 %stack.75.taps_ref = f32[8,9216]{1,0:T(8,128)} concatenate(f32[1,9216]{1,0:T(1,128)S(1)} %bitcast.106, f32[1,9216]{1,0:T(1,128)S(1)} %bitcast.105, f32[1,9216]{1,0:T(1,128)S(1)} %bitcast.104, f32[1,9216]{1,0:T(1,128)S(1)} %bitcast.103, f32[1,9216]{1,0:T(1,128)S(1)} %bitcast.102, f32[1,9216]{1,0:T(1,128)S(1)} %bitcast.101, f32[1,9216]{1,0:T(1,128)S(1)} %bitcast.100, ...), dimensions={0} | concatenate | bytes 589824 | tf_op jit(solution)/shard_map/stack | solution.py:234
  24.9 0.0 collective-permute-done
  24.9 0.1 pad.36
  25.1 0.7 copy.55
  25.8 19.6 %slot_bank.1 = (bf16[8,112,256]{2,1,0:T(8,128)(2,1)}, bf16[8,16,112]{2,1,0:T(8,128)(2,1)}) custom-call(s32[56]{0:T(128)} %min.12.pick_ref, bf16[2,270,3456]{2,1,0:T(8,128)(2,1)} %reshape_squeeze.3.x_ref, bf16[2,16,3456]{2,1,0:T(8,128)(2,1)} %bitcast.98, f32[8,9216]{1,0:T(8,128)} %stack.75.taps_ref, f32[512,384]{1,0:T(8,128)} %maximum_convert_fusion.rot_ref), custom_call_target="tpu_custom_call" | custom-call | tf_op jit(solution)/shard_map/slot_bank/pallas_call | solution.py:254
  45.4 17.4 %swap_slots.1 = (bf16[8,112,256]{2,1,0:T(8,128)(2,1)}, bf16[8,16,112]{2,1,0:T(8,128)(2,1)}) custom-call(bf16[8,112,256]{2,1,0:T(8,128)(2,1)} %get-tuple-element.9.in_ref, bf16[8,16,112]{2,1,0:T(8,128)(2,1)} %get-tuple-element.10.in_tail), custom_call_target="tpu_custom_call" | custom-call | tf_op jit(solution)/shard_map/swap_slots/pallas_call | solution.py:321
  62.8 0.9 %copy.33 = bf16[8,112,14]{2,1,0:T(8,128)(2,1)S(1)} copy(bf16[8,112,14]{1,2,0:T(8,128)(2,1)} %bitcast.107) | data formatting | bytes 50176 | tf_op jit(solution)/shard_map/slice | solution.py:333
  63.7 1.1 %pad_maximum_fusion = bf16[8,112,270]{2,1,0:T(8,128)(2,1)S(1)} fusion(bf16[8,112,14]{2,1,0:T(8,128)(2,1)S(1)} %copy.33, bf16[8,112,256]{2,1,0:T(8,128)(2,1)} %get-tuple-element.11), kind=kLoop, calls=%fused_computation.5 | loop fusion | flops 967680 | bytes 967680 | tf_op jit(solution)/shard_map/concatenate | solution.py:334
  64.8 0.1 copy.54
  65.0 2.3 %reshape.401 = bf16[2,7,8,5,432]{4,3,2,1,0:T(8,128)(2,1)S(1)} reshape(bf16[2,56,8,270]{3,2,1,0:T(8,128)(2,1)S(1)} %bitcast.96) | data formatting | bytes 967680 | tf_op jit(solution)/shard_map/reshape | solution.py:85
  67.3 1.6 %convert_reduce_fusion = bf16[2,7,8,432]{3,2,1,0:T(8,128)(2,1)S(1)} fusion(bf16[2,7,8,5,432]{4,3,2,1,0:T(8,128)(2,1)S(1)} %reshape.401, f32[8,432]{1,0:T(8,128)S(1)} %copy.38, f32[8,432]{1,0:T(8,128)S(1)} %copy.37, f32[8,432]{1,0:T(8,128)S(1)} %copy.36, f32[8,432]{1,0:T(8,128)S(1)} %copy.35, f32[8,432]{1,0:T(8,128)S(1)} %copy.31), kind=kLoop, calls=%fused_computation.27 | loop fusion | flops 725760 | bytes 649728 | tf_op jit(solution)/shard_map/convert_element_type | solution.py:93
  68.9 0.8 %reshape.402 = bf16[2,7,8,1,27,16]{5,4,2,1,0,3:T(8,128)(2,1)S(1)} reshape(bf16[2,7,8,432]{3,2,1,0:T(8,128)(2,1)S(1)} %convert_reduce_fusion) | data formatting | bytes 193536 | tf_op jit(solution)/shard_map/reshape | solution.py:93
  69.7 0.0 copy-start.2
  69.7 0.0 copy-start.3
  69.7 0.0 copy-start
  69.8 0.3 copy.48
  70.1 0.5 reshape.405
  70.7 0.2 convolution_bitcast_fusion.1
  70.9 0.0 copy-done.2
  70.9 0.0 copy-done.3
  71.0 0.2 convolution_bitcast_fusion
  71.2 0.3 copy.42
  71.5 0.7 reshape.404
  72.2 0.2 fusion.32
  72.3 0.1 pad_maximum_fusion.1
  72.5 0.1 fusion.22
  72.6 0.1 concatenate.32
  72.7 0.2 concatenate.33
  72.9 0.1 broadcast_multiply_fusion
  73.0 0.8 %copy.44 = f32[1,1,2,1,14580]{4,3,2,1,0:T(1,128)} copy(f32[1,1,2,1,14580]{4,2,3,1,0:T(2,128)S(1)} %broadcast_multiply_fusion) | data formatting | bytes 233280 | tf_op jit(solution)/shard_map/mul | solution.py:145
  (11 shorter events, 0.1 us)
Async XLA Ops:
  0.0 8.0 %copy-start.1 = (f32[5,3456]{1,0:T(8,128)S(1)}, f32[5,3456]{1,0:T(8,128)}, u32[]{:S(2)}) copy-start(f32[5,3456]{1,0:T(8,128)} %param.11) | copy-start | bytes 207364
  0.8 24.2 %collective-permute-start = (bf16[2,5712]{1,0:T(2,128)(2,1)S(1)}, bf16[2,5712]{1,0:T(2,128)(2,1)S(1)}, u32[]{:S(2)}, u32[]{:S(2)}) collective-permute-start(bf16[2,5712]{1,0:T(2,128)(2,1)S(1)} %slice.99), channel_id=1, source_target_pairs={{2,0},{4,2},{6,4},{8,6},{10,8},{12,10},{14,12},{3,1},{5,3},{7,5},{... | collective-permute-start | bytes 68552 | tf_op jit(solution)/shard_map/ppermute | solution.py:24
  8.7 3.5 %copy-start.4 = (s32[4,7]{1,0:T(4,128)S(1)}, s32[4,7]{1,0:T(4,128)}, u32[]{:S(2)}) copy-start(s32[4,7]{1,0:T(4,128)} %constant.117) | copy-start | bytes 340
  69.7 1.2 %copy-start.2 = (f32[27,128]{1,0:T(8,128)S(1)}, f32[27,128]{1,0:T(8,128)}, u32[]{:S(2)}) copy-start(f32[27,128]{1,0:T(8,128)} %constant.119) | copy-start | bytes 41476
  69.7 1.2 %copy-start.3 = (f32[27,128]{1,0:T(8,128)S(1)}, f32[27,128]{1,0:T(8,128)}, u32[]{:S(2)}) copy-start(f32[27,128]{1,0:T(8,128)} %constant.120) | copy-start | bytes 41476
  69.7 1.2 %copy-start = (bf16[256,2,128,1]{2,0,3,1:T(8,128)(2,1)S(1)}, bf16[256,2,128,1]{2,0,3,1:T(8,128)(2,1)}, u32[]{:S(2)}) copy-start(bf16[256,2,128,1]{2,0,3,1:T(8,128)(2,1)} %constant.121) | copy-start | bytes 393220
